TPU v7x, 512 devices: a whole 4x8x8 slice. The times are simulated.
512 devices in a mesh: dp: 4 (over x), expert: 32 (over z, y_lo), tensor: 4 (over y_hi, core).
Axes of the slice: x: 4, y: 8 (y_hi: 2, y_lo: 4; y = y_hi * 4 + y_lo), z: 8, core: 2. Of those that a mesh axis runs over, the one named last changes fastest.
Arguments:
- tokens: bfloat16 [16384, 7168], P(('dp', 'expert'), 'tensor'), may hold values from -6 to 6
- expert_ids: int32 [16384, 2], P(('dp', 'expert')), may hold values from 0 to 31, all different within a row; in each aligned block of 128 rows (0 to 127, 128 to 255, ...) at most 12 rows name the same one
- gate_scores: bfloat16 [16384, 2], P(('dp', 'expert')), may hold values from 0.099609375 to 0.59765625
- weight_in: bfloat16 [32, 2, 7168, 1024], P('expert', None, 'tensor', 'dp'), may hold values from -0.0625 to 0.0625
- weight_out: bfloat16 [32, 1024, 7168], P('expert', 'dp', 'tensor'), may hold values from -0.1875 to 0.1875
Outputs:
- mixed: bfloat16 [16384, 7168], P(('dp', 'expert'), 'tensor')
Inputs may be any that keep to these rules, and one draw needn't show every extreme that they name: `expert_ids`: each token names 2 different experts; among the 128 tokens of one index of dp and expert together (aligned blocks of rows) no expert is named more than 12 times, and in some blocks an expert is named exactly 12 times.
All inputs are finite; a program needn't handle non-finite values.
Results may differ from a plain program's by a relative error of at most 0.0071.
Values may be sent and summed in bfloat16 or wider, within the bound.
No kernel may reach another device: no remote copies, remote signals or barrier semaphores. Data moves between devices by JAX's collectives and lax.ppermute only.
A program may use at most 64 MiB of HBM per device.

v0:
```python
import jax
import jax.numpy as jnp
from jax import lax
from jax.sharding import Mesh
from jax.sharding import PartitionSpec as P

TENSOR = ("tensor_0", "tensor_1")


def one_axis_at_a_time(shard, axes):
    for axis in axes:
        shard = lax.psum(shard, axis)
    return shard


def in_blocks(shard, dim, devices):
    before, after = (shard.shape[:dim], shard.shape[dim + 1 :])
    return jnp.moveaxis(shard.reshape(*before, devices, -1, *after), dim, 0)


def sent_and_summed(shard, axis, dim):
    devices = lax.axis_size(axis)
    pieces = lax.all_to_all(in_blocks(shard, dim, devices), axis, 0, 0, tiled=True)
    return jnp.sum(pieces, axis=0)


def joined_along(pieces, dim):
    dims = list(pieces.shape[1:])
    dims[dim] *= pieces.shape[0]
    return jnp.moveaxis(pieces, 0, dim).reshape(dims)


def gather_in_order(shard, axes, order):
    pieces = shard[None]
    for k in order:
        pieces = lax.all_gather(pieces, axes[k], axis=0, tiled=True)
    held = [lax.axis_size(axes[k]) for k in reversed(order)]
    pieces = pieces.reshape(*held, *shard.shape)
    turned = sorted(range(len(order)), key=lambda place: order[len(order) - 1 - place])
    return pieces.transpose(*turned, *range(len(order), pieces.ndim)).reshape(-1, *shard.shape)


def gathered_by_axis(shard, axes, order, dim):
    return joined_along(gather_in_order(shard, axes, order), dim)


def per_device(tokens, expert_ids, gate_scores, weight_in, weight_out):
    experts = lax.axis_size("expert")
    tok_count, top_count = expert_ids.shape
    capacity = min(3 * tok_count * top_count // (2 * experts), tok_count)
    width_all = tokens.shape[1] * lax.axis_size(TENSOR)
    wide = tokens.astype(jnp.float32)
    row_squares = one_axis_at_a_time(jnp.sum(wide * wide, axis=1, keepdims=True), TENSOR)
    normed = (wide * lax.rsqrt(row_squares / width_all + 1e-06)).astype(jnp.bfloat16)
    flat_ids = expert_ids.reshape(-1)
    one_hot = (flat_ids[:, None] == jnp.arange(experts, dtype=jnp.int32)[None, :]).astype(jnp.int32)
    earlier = jnp.cumsum(one_hot, axis=0) - one_hot
    slot_pos = jnp.sum(earlier * one_hot, axis=1)
    target = flat_ids * capacity + slot_pos
    chosen = (target[:, None] == jnp.arange(experts * capacity, dtype=jnp.int32)[None, :]).astype(
        jnp.float32
    )
    chosen = chosen.reshape(tok_count, top_count, experts * capacity)
    picked = jnp.sum(chosen, axis=1).astype(jnp.bfloat16)
    combine_weight = jnp.sum(chosen * gate_scores.astype(jnp.float32)[:, :, None], axis=1).astype(
        jnp.bfloat16
    )
    outgoing = jnp.einsum("ts,td->sd", picked, normed, preferred_element_type=jnp.float32).astype(
        jnp.bfloat16
    )
    outgoing = outgoing.reshape(experts, capacity, tokens.shape[1])
    arrived = lax.all_to_all(outgoing, "expert", split_axis=0, concat_axis=0, tiled=True)
    slot_rows = arrived.reshape(experts * capacity, tokens.shape[1])
    local_in = weight_in[0]
    partial_sums = jnp.einsum(
        "rd,gdf->rgf",
        slot_rows,
        lax.all_gather(local_in, "dp", axis=2, tiled=True),
        preferred_element_type=jnp.float32,
    )
    summed = sent_and_summed(partial_sums, TENSOR, 2)
    hidden = (jax.nn.silu(summed[:, 0]) * summed[:, 1]).astype(jnp.bfloat16)
    hidden = hidden[:, None, :]
    row_count = hidden.shape[0]
    hidden_full = gathered_by_axis(hidden, TENSOR, (0, 1), 2).reshape(row_count, -1)
    expert_out = jnp.dot(
        hidden_full,
        lax.all_gather(weight_out[0], "dp", axis=0, tiled=True),
        preferred_element_type=jnp.float32,
    )
    sending = expert_out.astype(jnp.bfloat16).reshape(experts, capacity, weight_out.shape[2])
    returned = lax.all_to_all(sending, "expert", split_axis=0, concat_axis=0, tiled=True)
    mixed = jnp.dot(
        combine_weight,
        returned.reshape(experts * capacity, weight_out.shape[2]),
        preferred_element_type=jnp.float32,
    )
    return mixed.astype(jnp.bfloat16)


def solution(mesh):
    finer = Mesh(
        mesh.devices.reshape(mesh.shape["dp"], mesh.shape["expert"], 2, 2),
        ("dp", "expert", "tensor_0", "tensor_1"),
    )
    placed = (
        P(("dp", "expert"), TENSOR),
        P(("dp", "expert"), None),
        P(("dp", "expert"), None),
        P("expert", None, TENSOR, "dp"),
        P("expert", "dp", TENSOR),
    )
    return jax.shard_map(
        per_device,
        mesh=finer,
        in_specs=placed,
        out_specs=P(("dp", "expert"), TENSOR),
        check_vma=False,
    )
```

profile of v0, /device:TPU:6, one launch (start us, length us, event | category | flops | bytes accessed | tf_op | source)
XLA Modules:
  0.0 281.1 jit_solution(8761266857783817856)
XLA Ops:
  6.5 0.0 copy-start.1
  6.5 0.0 copy-start.2
  6.5 0.0 copy-start
  6.5 0.0 all-gather.5.cloned.1.call-start
  6.5 0.7 all-gather.5.cloned.1.call-update
  7.3 0.0 copy-done.1
  7.3 0.1 copy.47
  7.4 0.1 eq.39
  7.5 0.1 eq.43
  7.7 0.0 copy-done.2
  7.7 0.6 reduce-window.6
  8.3 0.2 slice_reduce_fusion
  8.5 0.1 fusion.16
  8.6 0.1 reduce_sum.48
  8.8 0.1 copy.50
  8.8 0.0 copy-done
  8.8 0.2 fusion.6
  9.0 8.8 %psum.14 = f32[128,1]{0,1:T(1,128)S(1)} all-reduce(f32[128,1]{0,1:T(1,128)S(1)} %bitcast.63), channel_id=1, replica_groups=mesh['dp'=4,'expert'=32,'tensor_0'=2,'tensor_1'=2] {'tensor_0'}, use_global_device_ids=true, to_apply=%region_6.7 | all-reduce | flops 128 | bytes 1024 | tf_op jit(solution)/shard_map/psum | solution.py:12
  17.9 2.4 psum.15
  20.3 0.1 select_reduce_fusion
  20.5 0.6 convolution_convert_fusion
  21.1 1.5 reshape.98
  22.6 13.7 %all-to-all-start = ((bf16[32,12,1792]{2,1,0:T(8,128)(2,1)}), bf16[32,12,1792]{2,1,0:T(8,128)(2,1)S(1)}, u32[]{:S(2)}, u32[]{:S(2)}) async-start(bf16[32,12,1792]{2,1,0:T(8,128)(2,1)} %reshape.98), calls=%async_computation | async-start | bytes 3670016 | tf_op jit(solution)/shard_map/all_to_all | solution.py:72
  36.3 0.0 all-gather.7.cloned.1.call-start
  36.4 0.7 all-gather.7.cloned.1.call-update
  37.1 45.9 %all-to-all-done = bf16[32,12,1792]{2,1,0:T(8,128)(2,1)S(1)} async-done(((bf16[32,12,1792]{2,1,0:T(8,128)(2,1)}), bf16[32,12,1792]{2,1,0:T(8,128)(2,1)S(1)}, u32[]{:S(2)}, u32[]{:S(2)}) %all-to-all-start) | async-done | bytes 1376288 | tf_op jit(solution)/shard_map/all_to_all | solution.py:72
  83.0 0.3 reshape.106
  83.4 14.0 %all-gather.5.cloned.1.call-done = bf16[1,2,1792,1024]{3,2,1,0:T(8,128)(2,1)} async-done(((bf16[1,2,1792,256]{3,2,1,0:T(8,128)(2,1)}), bf16[1,2,1792,1024]{3,2,1,0:T(8,128)(2,1)}) %all-gather.5.cloned.1.call-update) | async-done | bytes 7340048 | tf_op jit(solution)/shard_map/all_gather | solution.py:78
  97.3 10.1 %copy.51 = bf16[2,1024,1792]{2,1,0:T(8,128)(2,1)} copy(bf16[2,1024,1792]{1,2,0:T(8,128)(2,1)} %bitcast.58) | data formatting | bytes 14680064 | tf_op jit(solution)/shard_map/rd,gdf->rgf/dot_general | solution.py:75
  107.4 5.3 %convolution_bitcast_fusion = f32[4,384,2,256]{3,1,0,2:T(8,128)S(1)} fusion(bf16[2,4,256,1792]{3,2,1,0:T(8,128)(2,1)} %bitcast.59, bf16[384,1792,1,1]{1,0,2,3:T(8,128)(2,1)S(1)} %reshape.106), kind=kOutput, calls=%fused_computation.5 | convolution fusion | flops 2818572288 | bytes 11862016 | tf_op jit(solution)/shard_map/rd,gdf->rgf/dot_general | solution.py:75
  112.7 0.2 copy.52
  112.9 80.0 %all_to_all.15 = f32[4,384,2,256]{3,1,2,0:T(8,128)S(1)} all-to-all(f32[4,384,2,256]{3,1,2,0:T(8,128)S(1)} %copy.52), channel_id=1, replica_groups=mesh['dp'=4,'expert'=32,'tensor_0'=2,'tensor_1'=2] {'tensor_0','tensor_1'}, dimensions={0} | all-to-all | bytes 6291456 | tf_op jit(solution)/shard_map/all_to_all | solution.py:23
  192.9 1.2 reduce_sum.52
  194.0 1.2 fusion.11
  195.3 15.1 %all_gather.13 = bf16[2,384,1,256]{3,1,2,0:T(8,128)(2,1)S(1)} all-gather(bf16[1,384,1,256]{3,1,2,0:T(8,128)(2,1)S(1)} %fusion.11), channel_id=1, replica_groups=mesh['dp'=4,'expert'=32,'tensor_0'=2,'tensor_1'=2] {'tensor_0'}, dimensions={0}, use_global_device_ids=true | all-gather | bytes 589824 | tf_op jit(solution)/shard_map/all_gather | solution.py:36
  210.3 2.4 all_gather.14
  212.7 0.1 copy.53
  212.8 0.4 copy.54
  213.1 0.0 all-gather.7.cloned.1.call-done
  213.1 3.7 %fusion.2 = bf16[384,1792]{1,0:T(8,128)(2,1)S(1)} fusion(bf16[384,1024]{0,1:T(8,128)(2,1)S(1)} %bitcast.62, bf16[1,1024,1792]{2,1,0:T(8,128)(2,1)} %all-gather.7.cloned.1.call-done), kind=kOutput, calls=%fused_computation.3 | convolution fusion | flops 1409974272 | bytes 5832704 | tf_op jit(solution)/shard_map/dot_general | solution.py:86
  216.8 0.4 reshape.102
  217.2 53.5 %all_to_all.16 = bf16[32,12,1792]{2,1,0:T(8,128)(2,1)} all-to-all(bf16[32,12,1792]{2,1,0:T(8,128)(2,1)S(1)} %reshape.102), channel_id=1, replica_groups=mesh['dp'=4,'expert'=32,'tensor_0'=2,'tensor_1'=2] {'expert'}, dimensions={0} | all-to-all | bytes 2752512 | tf_op jit(solution)/shard_map/all_to_all | solution.py:92
  270.7 2.4 reshape.103
  273.1 1.2 convolution_convert_fusion.1
  (6 shorter events, 0.1 us)
Async XLA Ops:
  6.5 0.7 copy-start.1
  6.5 1.1 copy-start.2
  6.5 2.3 copy-start
  6.5 90.8 %all-gather.5.cloned.1.call-start = ((), (), s32[]{:S(2)}) async-start(), calls=%async_computation.3 | async-start | bytes 9175040 | tf_op jit(solution)/shard_map/all_gather | solution.py:78
  22.6 60.4 %all-to-all-start = ((bf16[32,12,1792]{2,1,0:T(8,128)(2,1)}), bf16[32,12,1792]{2,1,0:T(8,128)(2,1)S(1)}, u32[]{:S(2)}, u32[]{:S(2)}) async-start(bf16[32,12,1792]{2,1,0:T(8,128)(2,1)} %reshape.98), calls=%async_computation | async-start | bytes 3670016 | tf_op jit(solution)/shard_map/all_to_all | solution.py:72
  36.3 176.8 %all-gather.7.cloned.1.call-start = ((), (), s32[]{:S(2)}) async-start(), calls=%async_computation.4 | async-start | bytes 4587520 | tf_op jit(solution)/shard_map/all_gather | solution.py:88
Sparse Core Ops, SparseCore 0:
  9.5 87.8 all-gather.4
  99.4 48.5 all-gather.6
where the time goes:
time: 283 us; the launch traced here: 281 us
  blocking collectives  162 us (57%)
  waiting for transfers between devices  61.3 us (22%)
  local copies, waits for them, and re-layouts  16 us (6%)
  starting transfers between devices  13.8 us (5%)
  between operations  13.6 us (5%)
  matrix products  10.7 us (4%)
  other arithmetic  3.46 us (1%)
    all_to_all x1, blocking collectives, sent_and_summed(): lax.all_to_all(in_blocks(shard, dim, devices), axis, 0, 0, tiled=True)  80 us
    all_to_all x1, blocking collectives, per_device(): lax.all_to_all(sending, 'expert', split_axis=0, concat_axis=0, tiled=True)  53.5 us
    all_to_all x1, waiting for transfers between devices, per_device(): lax.all_to_all(outgoing, 'expert', split_axis=0, concat_axis=0, tiled=True)  45.9 us
    all_gather x2, blocking collectives, gather_in_order(): pieces = lax.all_gather(pieces, axes[k], axis=0, tiled=True)  17.4 us
    all_gather x1, waiting for transfers between devices, per_device(): lax.all_gather(local_in, 'dp', axis=2, tiled=True)  14 us
    all_to_all x1, starting transfers between devices, per_device(): lax.all_to_all(outgoing, 'expert', split_axis=0, concat_axis=0, tiled=True)  13.7 us
    psum x2, blocking collectives, one_axis_at_a_time(): shard = lax.psum(shard, axis)  11.3 us
    dot_general x1, local copies, waits for them, and re-layouts, per_device(): jnp.einsum('rd,gdf->rgf', slot_rows, lax.all_gather(local_in, 'dp', axis=...  10.1 us
  transfers between devices with their start and end apart: 3, of which 2 were waited for; matrix products, arithmetic and copies ran while one was open for 8% of the time, Pallas kernels for 0%

commit v1 on v0

v1 whole, which is shorter than its diff:
```python
import functools

import jax
import jax.numpy as jnp
from jax import lax
from jax.experimental import pallas as pl
from jax.experimental.pallas import tpu as pltpu
from jax.sharding import Mesh
from jax.sharding import PartitionSpec as P

INTERPRET = False
BF = jnp.bfloat16
F32 = jnp.float32
TENSOR = ("yh", "core")
FULL, EXTRA = 8, 4
VM = pl.BlockSpec(memory_space=pltpu.VMEM)
SM = pl.BlockSpec(memory_space=pltpu.SMEM)
HBM = pl.BlockSpec(memory_space=pltpu.HBM)


def kernel_call(body, out_shape, in_specs, out_specs, scratch=(), flops=0, moved=0):
    return pl.pallas_call(
        body,
        out_shape=out_shape,
        in_specs=in_specs,
        out_specs=out_specs,
        scratch_shapes=list(scratch),
        cost_estimate=pl.CostEstimate(flops=flops, transcendentals=0, bytes_accessed=moved),
        compiler_params=pltpu.CompilerParams(vmem_limit_bytes=16 << 20),
        interpret=INTERPRET,
    )


def in_hbm(x):
    return x if INTERPRET else pltpu.with_memory_space_constraint(x, pltpu.HBM)


def dot(a, b):
    return jnp.dot(a, b, preferred_element_type=F32)


def iota(shape, dim):
    return lax.broadcasted_iota(jnp.int32, shape, dim)


def fold_rows(extra_rows, part):
    row, col = iota((extra_rows, 2 * extra_rows), 0), iota((extra_rows, 2 * extra_rows), 1)
    return ((row // EXTRA) * FULL + EXTRA * part + row % EXTRA == col).astype(F32).astype(BF)


def unfold_rows(extra_rows, part):
    row, col = iota((2 * extra_rows, extra_rows), 0), iota((2 * extra_rows, extra_rows), 1)
    return ((col // EXTRA) * FULL + EXTRA * part + col % EXTRA == row).astype(F32).astype(BF)


def pack_body(ids_ref, tok_ref, out_ref, *, experts):
    count, width = tok_ref.shape
    half = width // 2
    ids = ids_ref[...]
    named = [iota((experts, count), 0) == ids[k : k + 1, :] for k in range(2)]
    members = (named[0] | named[1]).astype(F32)
    before = (iota((count, count), 0) < iota((count, count), 1)).astype(F32)
    earlier = dot(members.astype(BF), before.astype(BF))
    place = iota((experts * FULL, count), 0)
    whole = jnp.zeros((experts * FULL, count), F32)
    low = jnp.zeros((experts * FULL, count), F32)
    high = jnp.zeros((experts * FULL, count), F32)
    for k in range(2):
        slot = jnp.sum(jnp.where(named[k], earlier, 0.0), axis=0, keepdims=True).astype(jnp.int32)
        base = ids[k : k + 1, :] * FULL
        far = base + slot - FULL
        whole += jnp.where((place == base + slot) & (slot < FULL), 1.0, 0.0)
        low += jnp.where((place == far) & (slot >= FULL), 1.0, 0.0)
        high += jnp.where((place == far + EXTRA) & (slot >= FULL), 1.0, 0.0)
    tok = tok_ref[...]
    out_ref[:, :width] = dot(whole.astype(BF), tok).astype(BF)
    folded = dot(low.astype(BF), tok[:, :half]) + dot(high.astype(BF), tok[:, half:])
    out_ref[:, width:] = folded.astype(BF)


def mix_body(ids_ref, score_ref, back_ref, out_ref, *, experts):
    count, width = out_ref.shape
    half = width // 2
    ids = ids_ref[...]
    score = score_ref[...].astype(F32)
    named = [iota((count, experts), 1) == ids[:, k : k + 1] for k in range(2)]
    members = (named[0] | named[1]).astype(F32)
    before = (iota((count, count), 1) < iota((count, count), 0)).astype(F32)
    earlier = dot(before.astype(BF), members.astype(BF))
    place = iota((count, experts * FULL), 1)
    whole = jnp.zeros((count, experts * FULL), F32)
    low = jnp.zeros((count, experts * FULL), F32)
    high = jnp.zeros((count, experts * FULL), F32)
    for k in range(2):
        slot = jnp.sum(jnp.where(named[k], earlier, 0.0), axis=1, keepdims=True).astype(jnp.int32)
        base = ids[:, k : k + 1] * FULL
        far = base + slot - FULL
        gain = score[:, k : k + 1]
        whole += jnp.where((place == base + slot) & (slot < FULL), gain, 0.0)
        low += jnp.where((place == far) & (slot >= FULL), gain, 0.0)
        high += jnp.where((place == far + EXTRA) & (slot >= FULL), gain, 0.0)
    whole, low, high = whole.astype(BF), low.astype(BF), high.astype(BF)
    folded = back_ref[:, width:]
    out_ref[:, :half] = (dot(whole, back_ref[:, :half]) + dot(low, folded)).astype(BF)
    out_ref[:, half:] = (dot(whole, back_ref[:, half:width]) + dot(high, folded)).astype(BF)


def split_in_two(total, lanes):
    big = total.astype(BF).astype(F32)
    return jnp.where(iota((total.shape[0], lanes), 1) < lanes // 2, big, total - big)


def first_body(where_ref, arrived_ref, *refs):
    weights, (send_ref, keep_ref, rows_ref, extra, wbuf, sems) = refs[:6], refs[6:]
    slots, width = rows_ref.shape
    quarter = slots // 4
    fulls, extras = quarter * 2 // 3, quarter // 3
    half = width // 2
    cols = wbuf.shape[2]
    copies = [pltpu.make_async_copy(w, wbuf.at[i], sems.at[i]) for i, w in enumerate(weights)]
    for copy in copies:
        copy.start()
    folded = arrived_ref[:, width:]
    extra[:, :half] = dot(fold_rows(4 * extras, 0), folded).astype(BF)
    extra[:, half:] = dot(fold_rows(4 * extras, 1), folded).astype(BF)
    core, yh = where_ref[0], where_ref[1]
    for q in range(4):
        core_q = 1 - core if q < 2 else core
        yh_q = 1 - yh if q % 2 == 0 else yh
        owner = yh_q * 2 + core_q
        at = q * quarter
        rows_ref[at : at + fulls, :] = arrived_ref[pl.ds(pl.multiple_of(owner * fulls, fulls), fulls), :width]
        rows_ref[at + fulls : at + quarter, :] = extra[pl.ds(pl.multiple_of(owner * extras, extras), extras), :]
    middle = slots // 2
    for first, out_ref in ((0, send_ref), (middle, keep_ref)):
        part = rows_ref[first : first + middle, :].astype(F32)
        squares = jnp.sum(part * part, axis=1, keepdims=True)
        lanes = out_ref.shape[1] - 6 * cols
        out_ref[:, 6 * cols :] = split_in_two(squares, lanes).astype(out_ref.dtype)
    for i, copy in enumerate(copies):
        copy.wait()
        at = i * cols
        send_ref[:, at : at + cols] = dot(rows_ref[:middle, :], wbuf[i]).astype(BF)
        keep_ref[:, at : at + cols] = dot(rows_ref[middle:, :], wbuf[i])


def last_body(rows_ref, wg_ref, wu_ref, send_ref, keep_ref):
    middle = rows_ref.shape[0] // 2
    cols = wg_ref.shape[1]
    for g, w in enumerate((wg_ref, wu_ref)):
        send_ref[:, g * cols : (g + 1) * cols] = dot(rows_ref[:middle, :], w[...]).astype(BF)
        keep_ref[:, g * cols : (g + 1) * cols] = dot(rows_ref[middle:, :], w[...])


def halve_body(keep_ref, got_ref, send_ref, own_ref, *, lanes):
    part, total = send_ref.shape
    sums = total - lanes
    send_ref[:, :sums] = (keep_ref[:part, :sums] + got_ref[:part, :sums].astype(F32)).astype(BF)
    own_ref[:, :sums] = keep_ref[part:, :sums] + got_ref[part:, :sums].astype(F32)
    if lanes:
        pair = keep_ref[:, sums:] + got_ref[:, sums:].astype(F32)
        both = pair[:, :1] + pair[:, lanes // 2 : lanes // 2 + 1]
        split = split_in_two(both, lanes)
        send_ref[:, sums:] = split[:part].astype(BF)
        own_ref[:, sums:] = split[part:]


def silu_times(gate, up):
    return gate / (1.0 + jnp.exp(-gate)) * up


def act_first_body(own_ref, got_ref, hid_ref, scale_ref, *, width_all):
    lanes = scale_ref.shape[1]
    sums = own_ref.shape[1] - lanes
    cols = sums // 6
    pair = own_ref[:, sums:] + got_ref[:, sums:].astype(F32)
    squares = pair[:, :1] + pair[:, lanes // 2 : lanes // 2 + 1]
    scale = lax.rsqrt(squares * (1.0 / width_all) + 1e-06)
    scale_ref[...] = jnp.broadcast_to(scale, scale_ref.shape)
    for i in range(3):
        at = 2 * i * cols
        both = (own_ref[:, at : at + 2 * cols] + got_ref[:, at : at + 2 * cols].astype(F32)) * scale
        hid_ref[:, i * cols : (i + 1) * cols] = silu_times(both[:, :cols], both[:, cols:]).astype(BF)


def act_last_body(own_ref, got_ref, early_ref, scale_ref, hid_ref):
    cols = own_ref.shape[1] // 2
    both = (own_ref[...] + got_ref[...].astype(F32)) * scale_ref[:, :1]
    hid_ref[:, : 3 * cols] = early_ref[...]
    hid_ref[:, 3 * cols :] = silu_times(both[:, :cols], both[:, cols:]).astype(BF)


def down_body(where_ref, hid_ref, w_ref, out_ref, ha, hb, wbuf, sems):
    chunks, cols, width = w_ref.shape
    half = width // 2
    me = where_ref[2]
    copies = []
    for i, step in enumerate((0, 3, 1, 2)):
        source = lax.rem(me + step, 4)
        copies.append(pltpu.make_async_copy(w_ref.at[source], wbuf.at[pl.ds(i * cols, cols)], sems.at[i]))
    for copy in copies:
        copy.start()
    quarter = hid_ref.shape[0] // 4
    fulls, extras = quarter * 2 // 3, quarter // 3
    for t in range(4):
        ha[t * fulls : (t + 1) * fulls, :] = hid_ref[t * quarter : t * quarter + fulls, :]
        hb[t * extras : (t + 1) * extras, :] = hid_ref[t * quarter + fulls : (t + 1) * quarter, :]
    low = dot(unfold_rows(4 * extras, 0), hb[...]).astype(BF)
    high = dot(unfold_rows(4 * extras, 1), hb[...]).astype(BF)
    for copy in copies:
        copy.wait()
    out_ref[:, :width] = dot(ha[...], wbuf[...]).astype(BF)
    folded = dot(low, wbuf[:, :half]) + dot(high, wbuf[:, half:])
    out_ref[:, width:] = folded.astype(BF)


def shape(*dims, dtype=BF):
    return jax.ShapeDtypeStruct(dims, dtype)


def per_device(tokens, expert_ids, gate_scores, weight_in, weight_out):
    experts = lax.axis_size("z") * lax.axis_size("yl")
    count, width = tokens.shape
    width_all = width * lax.axis_size(TENSOR)
    cols = weight_in.shape[3]
    wire = width + width // 2
    slots = experts * (FULL + EXTRA)
    half, part = slots // 2, slots // 4
    lanes = 128
    first_cols = 6 * cols + lanes
    right = [(i, (i + 1) % 4) for i in range(4)]
    left = [(i, (i - 1) % 4) for i in range(4)]
    swap = [(0, 1), (1, 0)]
    where = jnp.stack([lax.axis_index("core"), lax.axis_index("yh"), lax.axis_index("dp")]).astype(jnp.int32)

    own_gate, own_up = weight_in[0, 0], weight_in[0, 1]
    left_gate = lax.ppermute(own_gate, "dp", right)
    right_up = lax.ppermute(own_up, "dp", left)
    left_up = lax.ppermute(own_up, "dp", right)
    right_gate = lax.ppermute(own_gate, "dp", left)
    far_gate = lax.ppermute(left_gate, "dp", right)
    far_up = lax.ppermute(right_up, "dp", left)

    outgoing = kernel_call(
        functools.partial(pack_body, experts=experts),
        shape(experts * FULL, wire),
        [VM, VM],
        VM,
        flops=4 * experts * FULL * count * width,
        moved=4 << 20,
    )(expert_ids.T, tokens)
    arrived = lax.all_to_all(outgoing.reshape(experts, FULL, wire), ("z", "yl"), 0, 0, tiled=True)
    arrived = arrived.reshape(experts * FULL, wire)

    send, keep, rows = kernel_call(
        first_body,
        (shape(half, first_cols), shape(half, first_cols, dtype=F32), shape(slots, width)),
        [SM, VM] + [HBM] * 6,
        (VM, VM, VM),
        (
            pltpu.VMEM((experts * EXTRA, width), BF),
            pltpu.VMEM((6, width, cols), BF),
            pltpu.SemaphoreType.DMA((6,)),
        ),
        flops=12 * slots * width * cols,
        moved=12 << 20,
    )(where, arrived, *map(in_hbm, (own_gate, own_up, left_gate, left_up, right_gate, right_up)))
    got = lax.ppermute(send, "core", swap)
    send, keep = kernel_call(
        functools.partial(halve_body, lanes=lanes),
        (shape(part, first_cols), shape(part, first_cols, dtype=F32)),
        [VM, VM],
        (VM, VM),
        moved=3 << 20,
    )(keep, got)
    got = lax.ppermute(send, "yh", swap)
    early, scale = kernel_call(
        functools.partial(act_first_body, width_all=width_all),
        (shape(part, 3 * cols), shape(part, lanes, dtype=F32)),
        [VM, VM],
        (VM, VM),
        moved=1 << 20,
    )(keep, got)

    send, keep = kernel_call(
        last_body,
        (shape(half, 2 * cols), shape(half, 2 * cols, dtype=F32)),
        [VM, VM, VM],
        (VM, VM),
        flops=4 * slots * width * cols,
        moved=4 << 20,
    )(rows, far_gate, far_up)
    got = lax.ppermute(send, "core", swap)
    send, keep = kernel_call(
        functools.partial(halve_body, lanes=0),
        (shape(part, 2 * cols), shape(part, 2 * cols, dtype=F32)),
        [VM, VM],
        (VM, VM),
        moved=1 << 20,
    )(keep, got)
    got = lax.ppermute(send, "yh", swap)
    hidden = kernel_call(
        act_last_body, shape(part, 4 * cols), [VM, VM, VM, VM], VM, moved=1 << 20
    )(keep, got, early, scale)

    hidden = lax.all_gather(hidden, TENSOR, axis=0, tiled=True)
    own_out = weight_out[0] + sum(x[:1, :1] for x in (arrived, left_gate, right_up, left_up, right_gate)) * 0
    down = lax.all_gather(own_out, "dp", axis=0)
    sending = kernel_call(
        down_body,
        shape(experts * FULL, wire),
        [SM, VM, HBM],
        VM,
        (
            pltpu.VMEM((experts * FULL, 4 * cols), BF),
            pltpu.VMEM((experts * EXTRA, 4 * cols), BF),
            pltpu.VMEM((4 * cols, width), BF),
            pltpu.SemaphoreType.DMA((4,)),
        ),
        flops=4 * experts * FULL * 4 * cols * width,
        moved=6 << 20,
    )(where, hidden, in_hbm(down))
    back = lax.all_to_all(sending.reshape(experts, FULL, wire), ("z", "yl"), 0, 0, tiled=True)
    return kernel_call(
        functools.partial(mix_body, experts=experts),
        shape(count, width),
        [VM, VM, VM],
        VM,
        flops=4 * experts * FULL * count * width,
        moved=2 << 20,
    )(expert_ids, gate_scores, back.reshape(experts * FULL, wire))


def solution(mesh):
    dp, expert = mesh.shape["dp"], mesh.shape["expert"]
    finer = Mesh(mesh.devices.reshape(dp, expert // 4, 4, 2, 2), ("dp", "z", "yl", "yh", "core"))
    group = ("dp", "z", "yl")
    placed = (
        P(group, TENSOR),
        P(group, None),
        P(group, None),
        P(("z", "yl"), None, TENSOR, "dp"),
        P(("z", "yl"), "dp", TENSOR),
    )
    return jax.shard_map(
        per_device, mesh=finer, in_specs=placed, out_specs=P(group, TENSOR), check_vma=False
    )
```

time: 283 us -> 207 us (0.73)
  blocking collectives: 162 us -> 11.6 us
  starting transfers between devices: 13.8 us -> 55.8 us
  waiting for transfers between devices: 61.3 us -> 97.9 us
  Pallas kernels: 0 us -> 16 us
  matrix products: 10.7 us -> 0 us
  local copies, waits for them, and re-layouts: 16 us -> 5.89 us
  between operations: 13.6 us -> 16.9 us
    all_to_all x2 -> x0, blocking collectives: 134 us -> none  [the longest x1 80 us: sent_and_summed(): lax.all_to_all(in_blocks(shard, dim, devices), axis, 0, 0, tiled=True)]
    ppermute x0 -> x10, waiting for transfers between devices: none -> 61.8 us  [the longest x1 14 us: per_device(): left_up = lax.ppermute(own_up, 'dp', right)]
    ppermute x0 -> x10, starting transfers between devices: none -> 29.3 us  [the longest x2 7.96 us: per_device(): got = lax.ppermute(send, 'yh', swap)]
    pallas_call x0 -> x9, Pallas kernels: none -> 16 us  [the longest x1 5.94 us: per_device(): kernel_call(down_body, shape(experts * FULL, wire), [SM, VM, HBM], VM, (p...]
    all_gather x2 -> x1, waiting for transfers between devices: 14 us -> 0.01 us  [per_device(): down = lax.all_gather(own_out, 'dp', axis=0)]
    all_to_all x1 -> x2, starting transfers between devices: 13.7 us -> 26.4 us  [the longest x1 13.9 us: per_device(): lax.all_to_all(outgoing.reshape(experts, FULL, wire), ('z', 'yl'), 0, 0,...]
    psum x2 -> x0, blocking collectives: 11.3 us -> none  [one_axis_at_a_time(): shard = lax.psum(shard, axis)]
    dot_general x4 -> x0, matrix products: 10.7 us -> none  [the longest x1 5.29 us: per_device(): jnp.einsum('rd,gdf->rgf', slot_rows, lax.all_gather(local_in, 'dp', axis=...]
  transfers between devices with their start and end apart: 3 -> 13, of which waited for: 2 -> 10; matrix products, arithmetic and copies ran while one was open for 8% -> 1% of each run, Pallas kernels for 0% -> 3%
where the time goes in v1:
time: 207 us; the launch traced here: 206 us
  waiting for transfers between devices  97.9 us (47%)
  starting transfers between devices  55.8 us (27%)
  between operations  16.9 us (8%)
  Pallas kernels  16 us (8%)
  blocking collectives  11.6 us (6%)
  local copies, waits for them, and re-layouts  5.89 us (3%)
  other arithmetic  2.24 us (1%)
    all_to_all x1, waiting for transfers between devices, per_device(): lax.all_to_all(sending.reshape(experts, FULL, wire), ('z', 'yl'), 0, 0, t...  36.1 us
    ppermute x1, waiting for transfers between devices, per_device(): left_up = lax.ppermute(own_up, 'dp', right)  14 us
    all_to_all x1, starting transfers between devices, per_device(): lax.all_to_all(outgoing.reshape(experts, FULL, wire), ('z', 'yl'), 0, 0,...  13.9 us
    ppermute x1, waiting for transfers between devices, per_device(): left_gate = lax.ppermute(own_gate, 'dp', right)  13.5 us
    all_to_all x1, starting transfers between devices, per_device(): lax.all_to_all(sending.reshape(experts, FULL, wire), ('z', 'yl'), 0, 0, t...  12.5 us
    all_gather x1, blocking collectives, per_device(): hidden = lax.all_gather(hidden, TENSOR, axis=0, tiled=True)  11.6 us
    ppermute x1, waiting for transfers between devices, per_device(): far_gate = lax.ppermute(left_gate, 'dp', right)  11.5 us
    ppermute x2, starting transfers between devices, per_device(): got = lax.ppermute(send, 'yh', swap)  7.96 us
  transfers between devices with their start and end apart: 13, of which 10 were waited for; matrix products, arithmetic and copies ran while one was open for 1% of the time, Pallas kernels for 3%

profile of v1, /device:TPU:6, one launch (start us, length us, event | category | flops | bytes accessed | tf_op | source)
XLA Modules:
  0.0 206.3 jit_solution(5810856206756595888)
XLA Ops:
  6.5 0.0 copy-start
  6.5 1.0 copy-done
  7.6 0.0 copy-start.1
  7.6 0.7 copy-done.1
  8.2 1.9 shard_map.55
  10.1 13.9 %all-to-all-start = ((bf16[32,8,2688]{2,1,0:T(8,128)(2,1)}), bf16[32,8,2688]{2,1,0:T(8,128)(2,1)S(1)}, u32[]{:S(2)}, u32[]{:S(2)}) async-start(bf16[32,8,2688]{2,1,0:T(8,128)(2,1)} %bitcast.4), calls=%async_computation | async-start | bytes 2752512 | tf_op jit(solution)/shard_map/all_to_all | solution.py:252
  24.0 0.0 all-gather.2.cloned.1.call-start
  24.0 0.0 copy-done.3
  24.0 0.1 slice_bitcast_fusion
  24.2 0.0 copy-start.4
  24.2 0.0 copy-start.5
  24.2 2.4 %collective-permute-start = (bf16[1792,256]{1,0:T(8,128)(2,1)S(1)}, bf16[1792,256]{1,0:T(8,128)(2,1)S(1)}, u32[]{:S(2)}, u32[]{:S(2)}) collective-permute-start(bf16[1792,256]{1,0:T(8,128)(2,1)S(1)} %get-tuple-element.28.refs_0_), channel_id=1, source_target_pairs={{0,128},{128,256},{256,384},{384,0},{1,129},{129,257},{257,385},{3... | collective-permute-start | bytes 2752520 | tf_op jit(solution)/shard_map/ppermute | solution.py:237
  26.6 3.5 %collective-permute-start.3 = (bf16[1792,256]{1,0:T(8,128)(2,1)S(1)}, bf16[1792,256]{1,0:T(8,128)(2,1)S(1)}, u32[]{:S(2)}, u32[]{:S(2)}) collective-permute-start(bf16[1792,256]{1,0:T(8,128)(2,1)S(1)} %get-tuple-element.27.refs_1_), channel_id=1, source_target_pairs={{0,384},{128,0},{256,128},{384,256},{1,385},{129,1},{257,129},{385... | collective-permute-start | bytes 2752520 | tf_op jit(solution)/shard_map/ppermute | solution.py:238
  30.0 3.6 %collective-permute-start.1 = (bf16[1792,256]{1,0:T(8,128)(2,1)S(1)}, bf16[1792,256]{1,0:T(8,128)(2,1)S(1)}, u32[]{:S(2)}, u32[]{:S(2)}) collective-permute-start(bf16[1792,256]{1,0:T(8,128)(2,1)S(1)} %get-tuple-element.27.refs_1_), channel_id=1, source_target_pairs={{0,128},{128,256},{256,384},{384,0},{1,129},{129,257},{257,385},{3... | collective-permute-start | bytes 2752520 | tf_op jit(solution)/shard_map/ppermute | solution.py:239
  33.7 2.2 %collective-permute-start.2 = (bf16[1792,256]{1,0:T(8,128)(2,1)S(1)}, bf16[1792,256]{1,0:T(8,128)(2,1)S(1)}, u32[]{:S(2)}, u32[]{:S(2)}) collective-permute-start(bf16[1792,256]{1,0:T(8,128)(2,1)S(1)} %get-tuple-element.28.refs_0_), channel_id=1, source_target_pairs={{0,384},{128,0},{256,128},{384,256},{1,385},{129,1},{257,129},{385... | collective-permute-start | bytes 2752520 | tf_op jit(solution)/shard_map/ppermute | solution.py:240
  35.9 13.5 %collective-permute-done.refs_2_ = bf16[1792,256]{1,0:T(8,128)(2,1)S(1)} collective-permute-done((bf16[1792,256]{1,0:T(8,128)(2,1)S(1)}, bf16[1792,256]{1,0:T(8,128)(2,1)S(1)}, u32[]{:S(2)}, u32[]{:S(2)}) %collective-permute-start) | collective-permute-done | bytes 917536 | tf_op jit(solution)/shard_map/ppermute | solution.py:237
  49.4 0.0 copy-start.7
  49.4 0.5 slice.29
  49.9 3.1 %collective-permute-done.3.refs_5_ = bf16[1792,256]{1,0:T(8,128)(2,1)S(1)} collective-permute-done((bf16[1792,256]{1,0:T(8,128)(2,1)S(1)}, bf16[1792,256]{1,0:T(8,128)(2,1)S(1)}, u32[]{:S(2)}, u32[]{:S(2)}) %collective-permute-start.3) | collective-permute-done | bytes 917536 | tf_op jit(solution)/shard_map/ppermute | solution.py:238
  53.0 0.6 slice.30
  53.6 14.0 %collective-permute-done.1.refs_3_ = bf16[1792,256]{1,0:T(8,128)(2,1)S(1)} collective-permute-done((bf16[1792,256]{1,0:T(8,128)(2,1)S(1)}, bf16[1792,256]{1,0:T(8,128)(2,1)S(1)}, u32[]{:S(2)}, u32[]{:S(2)}) %collective-permute-start.1) | collective-permute-done | bytes 917536 | tf_op jit(solution)/shard_map/ppermute | solution.py:239
  67.6 0.6 slice.31
  68.1 2.8 %collective-permute-done.2.refs_4_ = bf16[1792,256]{1,0:T(8,128)(2,1)S(1)} collective-permute-done((bf16[1792,256]{1,0:T(8,128)(2,1)S(1)}, bf16[1792,256]{1,0:T(8,128)(2,1)S(1)}, u32[]{:S(2)}, u32[]{:S(2)}) %collective-permute-start.2) | collective-permute-done | bytes 917536 | tf_op jit(solution)/shard_map/ppermute | solution.py:240
  70.9 0.0 copy-done.4
  70.9 0.0 copy-done.5
  70.9 0.0 copy-done.9
  70.9 0.0 copy-start.10
  70.9 1.0 copy-done.10
  71.9 0.6 slice.32
  72.5 0.0 all-to-all-done
  72.5 0.5 slice.28
  76.2 2.2 %broadcast_add_fusion = bf16[1,256,1792]{2,1,0:T(8,128)(2,1)} fusion(bf16[1,256,1792]{2,1,0:T(8,128)(2,1)} %param.9, bf16[]{:T(256)} %bitcast.8), kind=kLoop, calls=%fused_computation.2 | loop fusion | flops 458752 | bytes 1835010 | tf_op jit(solution)/shard_map/add | solution.py:307
  78.3 0.0 all-gather.2.cloned.1.call-update
  78.4 0.0 copy-done.7
  78.4 2.2 %collective-permute-start.4 = (bf16[1792,256]{1,0:T(8,128)(2,1)S(1)}, bf16[1792,256]{1,0:T(8,128)(2,1)S(1)}, u32[]{:S(2)}, u32[]{:S(2)}) collective-permute-start(bf16[1792,256]{1,0:T(8,128)(2,1)S(1)} %collective-permute-done.refs_2_), channel_id=1, source_target_pairs={{0,128},{128,256},{256,384},{384,0},{1,129},{129,257},{257,385},{3... | collective-permute-start | bytes 2752520 | tf_op jit(solution)/shard_map/ppermute | solution.py:241
  80.6 0.0 copy-done.8
  80.6 3.7 %collective-permute-start.5 = (bf16[1792,256]{1,0:T(8,128)(2,1)S(1)}, bf16[1792,256]{1,0:T(8,128)(2,1)S(1)}, u32[]{:S(2)}, u32[]{:S(2)}) collective-permute-start(bf16[1792,256]{1,0:T(8,128)(2,1)S(1)} %collective-permute-done.3.refs_5_), channel_id=1, source_target_pairs={{0,384},{128,0},{256,128},{384,256},{1,385},{129,1},{257,129},{385... | collective-permute-start | bytes 2752520 | tf_op jit(solution)/shard_map/ppermute | solution.py:242
  84.3 0.1 pad_add_fusion.where_ref
  84.3 5.0 %shard_map.56 = (bf16[192,1664]{1,0:T(8,128)(2,1)S(1)}, f32[192,1664]{1,0:T(8,128)S(1)}, bf16[384,1792]{1,0:T(8,128)(2,1)S(1)}) custom-call(s32[3]{0:T(128)S(1)} %pad_add_fusion.where_ref, bf16[256,2688]{1,0:T(8,128)(2,1)S(1)} %bitcast.15, bf16[1792,256]{1,0:T(8,128)(2,1)} %copy-done.5, bf16[1792,256]{1,0:T(8,128)(2,1)} %copy-done.4, ...), custom_call_target="tpu_custom_call" | custom-call | flops 2113929216 | bytes 12582912 | tf_op jit(solution)/shard_map/pallas_call | solution.py:255
  89.4 1.9 collective-permute-start.8
  91.3 2.0 collective-permute-done.8.got_ref
  93.3 0.3 shard_map.59
  93.6 5.0 %collective-permute-start.9 = (bf16[96,1664]{1,0:T(8,128)(2,1)S(1)}, bf16[96,1664]{1,0:T(8,128)(2,1)S(1)}, u32[]{:S(2)}, u32[]{:S(2)}) collective-permute-start(bf16[96,1664]{1,0:T(8,128)(2,1)S(1)} %get-tuple-element.24), channel_id=1, source_target_pairs={{0,2},{2,0},{1,3},{3,1},{4,6},{6,4},{5,7},{7,5},{8,10},{10,8},{9,1... | collective-permute-start | bytes 958472 | tf_op jit(solution)/shard_map/ppermute | solution.py:276
  98.6 11.5 %collective-permute-done.4.wg_ref = bf16[1792,256]{1,0:T(8,128)(2,1)S(1)} collective-permute-done((bf16[1792,256]{1,0:T(8,128)(2,1)S(1)}, bf16[1792,256]{1,0:T(8,128)(2,1)S(1)}, u32[]{:S(2)}, u32[]{:S(2)}) %collective-permute-start.4) | collective-permute-done | bytes 917536 | tf_op jit(solution)/shard_map/ppermute | solution.py:241
  110.1 6.1 %collective-permute-done.5.wu_ref = bf16[1792,256]{1,0:T(8,128)(2,1)S(1)} collective-permute-done((bf16[1792,256]{1,0:T(8,128)(2,1)S(1)}, bf16[1792,256]{1,0:T(8,128)(2,1)S(1)}, u32[]{:S(2)}, u32[]{:S(2)}) %collective-permute-start.5) | collective-permute-done | bytes 917536 | tf_op jit(solution)/shard_map/ppermute | solution.py:242
  116.2 0.9 shard_map.57
  117.1 1.9 collective-permute-start.6
  119.0 1.4 collective-permute-done.6.got_ref
  120.5 3.0 %collective-permute-start.7 = (bf16[96,512]{1,0:T(8,128)(2,1)S(1)}, bf16[96,512]{1,0:T(8,128)(2,1)S(1)}, u32[]{:S(2)}, u32[]{:S(2)}) collective-permute-start(bf16[96,512]{1,0:T(8,128)(2,1)S(1)} %get-tuple-element.20), channel_id=1, source_target_pairs={{0,2},{2,0},{1,3},{3,1},{4,6},{6,4},{5,7},{7,5},{8,10},{10,8},{9,1... | collective-permute-start | bytes 294920 | tf_op jit(solution)/shard_map/ppermute | solution.py:301
  123.4 0.0 collective-permute-done.9.got_ref
  123.5 0.2 shard_map.60
  123.7 7.5 %collective-permute-done.7.got_ref = bf16[96,512]{1,0:T(8,128)(2,1)S(1)} collective-permute-done((bf16[96,512]{1,0:T(8,128)(2,1)S(1)}, bf16[96,512]{1,0:T(8,128)(2,1)S(1)}, u32[]{:S(2)}, u32[]{:S(2)}) %collective-permute-start.7) | collective-permute-done | bytes 98336 | tf_op jit(solution)/shard_map/ppermute | solution.py:301
  131.2 0.1 shard_map.61
  131.3 11.6 %all_gather.7.hid_ref = bf16[384,1024]{1,0:T(8,128)(2,1)S(1)} all-gather(bf16[96,1024]{1,0:T(8,128)(2,1)S(1)} %shard_map.61), channel_id=1, replica_groups=mesh['dp'=4,'z'=8,'yl'=4,'yh'=2,'core'=2] {'yh','core'}, dimensions={0}, use_global_device_ids=true | all-gather | bytes 983040 | tf_op jit(solution)/shard_map/all_gather | solution.py:306
  142.9 5.9 %shard_map.62 = bf16[256,2688]{1,0:T(8,128)(2,1)} custom-call(s32[3]{0:T(128)S(1)} %pad_add_fusion.where_ref, bf16[384,1024]{1,0:T(8,128)(2,1)S(1)} %all_gather.7.hid_ref, bf16[4,256,1792]{2,1,0:T(8,128)(2,1)} %all-gather.2.cloned.1.call-done.w_ref), custom_call_target="tpu_custom_call" | custom-call | flops 1879048192 | bytes 6291456 | tf_op jit(solution)/shard_map/pallas_call | solution.py:309
  148.9 0.0 copy-start.2
  148.9 0.0 copy-start.6
  148.9 12.5 %all-to-all-start.1 = ((bf16[32,8,2688]{2,1,0:T(8,128)(2,1)}), bf16[32,8,2688]{2,1,0:T(8,128)(2,1)S(1)}, u32[]{:S(2)}, u32[]{:S(2)}) async-start(bf16[32,8,2688]{2,1,0:T(8,128)(2,1)} %bitcast.9), calls=%async_computation.1 | async-start | bytes 2752512 | tf_op jit(solution)/shard_map/all_to_all | solution.py:323
  161.4 0.0 copy-done.2
  161.4 0.1 copy.8.ids_ref
  161.5 0.0 copy-done.6
  161.6 0.1 copy.9.score_ref
  161.7 36.1 %all-to-all-done.1 = bf16[32,8,2688]{2,1,0:T(8,128)(2,1)S(1)} async-done(((bf16[32,8,2688]{2,1,0:T(8,128)(2,1)}), bf16[32,8,2688]{2,1,0:T(8,128)(2,1)S(1)}, u32[]{:S(2)}, u32[]{:S(2)}) %all-to-all-start.1) | async-done | bytes 1376288 | tf_op jit(solution)/shard_map/all_to_all | solution.py:323
  197.8 1.7 shard_map.63
  (5 shorter events, 0.0 us)
Async XLA Ops:
  6.5 1.0 copy-start
  7.6 0.7 copy-start.1
  10.1 13.9 %copy-start.3 = (bf16[1,2,1792,256]{3,2,1,0:T(8,128)(2,1)S(1)}, bf16[1,2,1792,256]{3,2,1,0:T(8,128)(2,1)}, u32[]{:S(2)}) copy-start(bf16[1,2,1792,256]{3,2,1,0:T(8,128)(2,1)} %param.8) | copy-start | bytes 5505028
  10.1 62.4 %all-to-all-start = ((bf16[32,8,2688]{2,1,0:T(8,128)(2,1)}), bf16[32,8,2688]{2,1,0:T(8,128)(2,1)S(1)}, u32[]{:S(2)}, u32[]{:S(2)}) async-start(bf16[32,8,2688]{2,1,0:T(8,128)(2,1)} %bitcast.4), calls=%async_computation | async-start | bytes 2752512 | tf_op jit(solution)/shard_map/all_to_all | solution.py:252
  24.0 119.0 %all-gather.2.cloned.1.call-start = ((), (), s32[]{:S(2)}) async-start(), calls=%async_computation.2 | async-start | bytes 4587520 | tf_op jit(solution)/shard_map/all_gather | solution.py:308
  24.2 46.7 %copy-start.4 = (bf16[1792,256]{1,0:T(8,128)(2,1)}, bf16[1792,256]{1,0:T(8,128)(2,1)S(1)}, u32[]{:S(2)}) copy-start(bf16[1792,256]{1,0:T(8,128)(2,1)S(1)} %get-tuple-element.27.refs_1_) | copy-start | bytes 2752516
  24.2 46.7 %copy-start.5 = (bf16[1792,256]{1,0:T(8,128)(2,1)}, bf16[1792,256]{1,0:T(8,128)(2,1)S(1)}, u32[]{:S(2)}) copy-start(bf16[1792,256]{1,0:T(8,128)(2,1)S(1)} %get-tuple-element.28.refs_0_) | copy-start | bytes 2752516
  24.2 25.2 %collective-permute-start = (bf16[1792,256]{1,0:T(8,128)(2,1)S(1)}, bf16[1792,256]{1,0:T(8,128)(2,1)S(1)}, u32[]{:S(2)}, u32[]{:S(2)}) collective-permute-start(bf16[1792,256]{1,0:T(8,128)(2,1)S(1)} %get-tuple-element.28.refs_0_), channel_id=1, source_target_pairs={{0,128},{128,256},{256,384},{384,0},{1,129},{129,257},{257,385},{3... | collective-permute-start | bytes 2752520 | tf_op jit(solution)/shard_map/ppermute | solution.py:237
  26.6 26.4 %collective-permute-start.3 = (bf16[1792,256]{1,0:T(8,128)(2,1)S(1)}, bf16[1792,256]{1,0:T(8,128)(2,1)S(1)}, u32[]{:S(2)}, u32[]{:S(2)}) collective-permute-start(bf16[1792,256]{1,0:T(8,128)(2,1)S(1)} %get-tuple-element.27.refs_1_), channel_id=1, source_target_pairs={{0,384},{128,0},{256,128},{384,256},{1,385},{129,1},{257,129},{385... | collective-permute-start | bytes 2752520 | tf_op jit(solution)/shard_map/ppermute | solution.py:238
  30.0 37.5 %collective-permute-start.1 = (bf16[1792,256]{1,0:T(8,128)(2,1)S(1)}, bf16[1792,256]{1,0:T(8,128)(2,1)S(1)}, u32[]{:S(2)}, u32[]{:S(2)}) collective-permute-start(bf16[1792,256]{1,0:T(8,128)(2,1)S(1)} %get-tuple-element.27.refs_1_), channel_id=1, source_target_pairs={{0,128},{128,256},{256,384},{384,0},{1,129},{129,257},{257,385},{3... | collective-permute-start | bytes 2752520 | tf_op jit(solution)/shard_map/ppermute | solution.py:239
  33.7 37.2 %collective-permute-start.2 = (bf16[1792,256]{1,0:T(8,128)(2,1)S(1)}, bf16[1792,256]{1,0:T(8,128)(2,1)S(1)}, u32[]{:S(2)}, u32[]{:S(2)}) collective-permute-start(bf16[1792,256]{1,0:T(8,128)(2,1)S(1)} %get-tuple-element.28.refs_0_), channel_id=1, source_target_pairs={{0,384},{128,0},{256,128},{384,256},{1,385},{129,1},{257,129},{385... | collective-permute-start | bytes 2752520 | tf_op jit(solution)/shard_map/ppermute | solution.py:240
  49.4 29.0 %copy-start.7 = (bf16[1792,256]{1,0:T(8,128)(2,1)}, bf16[1792,256]{1,0:T(8,128)(2,1)S(1)}, u32[]{:S(2)}) copy-start(bf16[1792,256]{1,0:T(8,128)(2,1)S(1)} %collective-permute-done.refs_2_) | copy-start | bytes 2752516
  53.0 27.6 %copy-start.8 = (bf16[1792,256]{1,0:T(8,128)(2,1)}, bf16[1792,256]{1,0:T(8,128)(2,1)S(1)}, u32[]{:S(2)}) copy-start(bf16[1792,256]{1,0:T(8,128)(2,1)S(1)} %collective-permute-done.3.refs_5_) | copy-start | bytes 2752516
  67.6 3.3 %copy-start.9 = (bf16[1792,256]{1,0:T(8,128)(2,1)}, bf16[1792,256]{1,0:T(8,128)(2,1)S(1)}, u32[]{:S(2)}) copy-start(bf16[1792,256]{1,0:T(8,128)(2,1)S(1)} %collective-permute-done.1.refs_3_) | copy-start | bytes 2752516
  70.9 1.0 copy-start.10
  78.4 31.8 %collective-permute-start.4 = (bf16[1792,256]{1,0:T(8,128)(2,1)S(1)}, bf16[1792,256]{1,0:T(8,128)(2,1)S(1)}, u32[]{:S(2)}, u32[]{:S(2)}) collective-permute-start(bf16[1792,256]{1,0:T(8,128)(2,1)S(1)} %collective-permute-done.refs_2_), channel_id=1, source_target_pairs={{0,128},{128,256},{256,384},{384,0},{1,129},{129,257},{257,385},{3... | collective-permute-start | bytes 2752520 | tf_op jit(solution)/shard_map/ppermute | solution.py:241
  80.6 35.6 %collective-permute-start.5 = (bf16[1792,256]{1,0:T(8,128)(2,1)S(1)}, bf16[1792,256]{1,0:T(8,128)(2,1)S(1)}, u32[]{:S(2)}, u32[]{:S(2)}) collective-permute-start(bf16[1792,256]{1,0:T(8,128)(2,1)S(1)} %collective-permute-done.3.refs_5_), channel_id=1, source_target_pairs={{0,384},{128,0},{256,128},{384,256},{1,385},{129,1},{257,129},{385... | collective-permute-start | bytes 2752520 | tf_op jit(solution)/shard_map/ppermute | solution.py:242
  89.4 4.0 %collective-permute-start.8 = (bf16[192,1664]{1,0:T(8,128)(2,1)S(1)}, bf16[192,1664]{1,0:T(8,128)(2,1)S(1)}, u32[]{:S(2)}, u32[]{:S(2)}) collective-permute-start(bf16[192,1664]{1,0:T(8,128)(2,1)S(1)} %get-tuple-element.22), channel_id=1, source_target_pairs={{0,1},{1,0},{2,3},{3,2},{4,5},{5,4},{6,7},{7,6},{8,9},{9,8},{10,11... | collective-permute-start | bytes 1916936 | tf_op jit(solution)/shard_map/ppermute | solution.py:268
  93.6 29.9 %collective-permute-start.9 = (bf16[96,1664]{1,0:T(8,128)(2,1)S(1)}, bf16[96,1664]{1,0:T(8,128)(2,1)S(1)}, u32[]{:S(2)}, u32[]{:S(2)}) collective-permute-start(bf16[96,1664]{1,0:T(8,128)(2,1)S(1)} %get-tuple-element.24), channel_id=1, source_target_pairs={{0,2},{2,0},{1,3},{3,1},{4,6},{6,4},{5,7},{7,5},{8,10},{10,8},{9,1... | collective-permute-start | bytes 958472 | tf_op jit(solution)/shard_map/ppermute | solution.py:276
  117.1 3.3 %collective-permute-start.6 = (bf16[192,512]{1,0:T(8,128)(2,1)S(1)}, bf16[192,512]{1,0:T(8,128)(2,1)S(1)}, u32[]{:S(2)}, u32[]{:S(2)}) collective-permute-start(bf16[192,512]{1,0:T(8,128)(2,1)S(1)} %get-tuple-element.18), channel_id=1, source_target_pairs={{0,1},{1,0},{2,3},{3,2},{4,5},{5,4},{6,7},{7,6},{8,9},{9,8},{10,11... | collective-permute-start | bytes 589832 | tf_op jit(solution)/shard_map/ppermute | solution.py:293
  120.5 10.7 %collective-permute-start.7 = (bf16[96,512]{1,0:T(8,128)(2,1)S(1)}, bf16[96,512]{1,0:T(8,128)(2,1)S(1)}, u32[]{:S(2)}, u32[]{:S(2)}) collective-permute-start(bf16[96,512]{1,0:T(8,128)(2,1)S(1)} %get-tuple-element.20), channel_id=1, source_target_pairs={{0,2},{2,0},{1,3},{3,1},{4,6},{6,4},{5,7},{7,5},{8,10},{10,8},{9,1... | collective-permute-start | bytes 294920 | tf_op jit(solution)/shard_map/ppermute | solution.py:301
  148.9 12.5 %copy-start.2 = (s32[128,2]{0,1:T(2,128)S(1)}, s32[128,2]{0,1:T(2,128)}, u32[]{:S(2)}) copy-start(s32[128,2]{0,1:T(2,128)} %param.6) | copy-start | bytes 3076
  148.9 12.7 %copy-start.6 = (bf16[128,2]{0,1:T(2,128)(2,1)S(1)}, bf16[128,2]{0,1:T(2,128)(2,1)}, u32[]{:S(2)}) copy-start(bf16[128,2]{0,1:T(2,128)(2,1)} %param.7) | copy-start | bytes 1540
  148.9 48.9 %all-to-all-start.1 = ((bf16[32,8,2688]{2,1,0:T(8,128)(2,1)}), bf16[32,8,2688]{2,1,0:T(8,128)(2,1)S(1)}, u32[]{:S(2)}, u32[]{:S(2)}) async-start(bf16[32,8,2688]{2,1,0:T(8,128)(2,1)} %bitcast.9), calls=%async_computation.1 | async-start | bytes 2752512 | tf_op jit(solution)/shard_map/all_to_all | solution.py:323
Sparse Core Ops, SparseCore 0:
  78.5 55.3 all-gather.1

commit v2 on v1

--- a/solution.py
+++ b/solution.py
@@ -111,13 +111,13 @@
 
 
 def first_body(where_ref, arrived_ref, *refs):
-    weights, (send_ref, keep_ref, rows_ref, extra, wbuf, sems) = refs[:6], refs[6:]
+    weights, (send_ref, keep_ref, rows_ref, extra, wbuf, sems) = refs[:3], refs[3:]
     slots, width = rows_ref.shape
     quarter = slots // 4
     fulls, extras = quarter * 2 // 3, quarter // 3
     half = width // 2
     cols = wbuf.shape[2]
-    copies = [pltpu.make_async_copy(w, wbuf.at[i], sems.at[i]) for i, w in enumerate(weights)]
+    copies = [pltpu.make_async_copy(w, wbuf.at[pl.ds(2 * i, 2)], sems.at[i]) for i, w in enumerate(weights)]
     for copy in copies:
         copy.start()
     folded = arrived_ref[:, width:]
@@ -139,9 +139,10 @@
         out_ref[:, 6 * cols :] = split_in_two(squares, lanes).astype(out_ref.dtype)
     for i, copy in enumerate(copies):
         copy.wait()
-        at = i * cols
-        send_ref[:, at : at + cols] = dot(rows_ref[:middle, :], wbuf[i]).astype(BF)
-        keep_ref[:, at : at + cols] = dot(rows_ref[middle:, :], wbuf[i])
+        for at in range(2 * i, 2 * i + 2):
+            to = slice(at * cols, (at + 1) * cols)
+            send_ref[:, to] = dot(rows_ref[:middle, :], wbuf[at]).astype(BF)
+            keep_ref[:, to] = dot(rows_ref[middle:, :], wbuf[at])
 
 
 def last_body(rows_ref, wg_ref, wu_ref, send_ref, keep_ref):
@@ -233,20 +234,18 @@
     swap = [(0, 1), (1, 0)]
     where = jnp.stack([lax.axis_index("core"), lax.axis_index("yh"), lax.axis_index("dp")]).astype(jnp.int32)
 
-    own_gate, own_up = weight_in[0, 0], weight_in[0, 1]
-    left_gate = lax.ppermute(own_gate, "dp", right)
-    right_up = lax.ppermute(own_up, "dp", left)
-    left_up = lax.ppermute(own_up, "dp", right)
-    right_gate = lax.ppermute(own_gate, "dp", left)
-    far_gate = lax.ppermute(left_gate, "dp", right)
-    far_up = lax.ppermute(right_up, "dp", left)
+    own_in = weight_in[0]
+    from_left = lax.ppermute(own_in, "dp", right)
+    from_right = lax.ppermute(own_in, "dp", left)
+    far_gate = lax.ppermute(from_left[0], "dp", right)
+    far_up = lax.ppermute(from_right[1], "dp", left)
 
     outgoing = kernel_call(
         functools.partial(pack_body, experts=experts),
         shape(experts * FULL, wire),
         [VM, VM],
         VM,
-        flops=4 * experts * FULL * count * width,
+        flops=1 * 4 * experts * FULL * count * width,
         moved=4 << 20,
     )(expert_ids.T, tokens)
     arrived = lax.all_to_all(outgoing.reshape(experts, FULL, wire), ("z", "yl"), 0, 0, tiled=True)
@@ -255,16 +254,16 @@
     send, keep, rows = kernel_call(
         first_body,
         (shape(half, first_cols), shape(half, first_cols, dtype=F32), shape(slots, width)),
-        [SM, VM] + [HBM] * 6,
+        [SM, VM] + [HBM] * 3,
         (VM, VM, VM),
         (
             pltpu.VMEM((experts * EXTRA, width), BF),
             pltpu.VMEM((6, width, cols), BF),
-            pltpu.SemaphoreType.DMA((6,)),
+            pltpu.SemaphoreType.DMA((3,)),
         ),
-        flops=12 * slots * width * cols,
+        flops=100 * 12 * slots * width * cols,
         moved=12 << 20,
-    )(where, arrived, *map(in_hbm, (own_gate, own_up, left_gate, left_up, right_gate, right_up)))
+    )(where, arrived, *map(in_hbm, (own_in, from_left, from_right)))
     got = lax.ppermute(send, "core", swap)
     send, keep = kernel_call(
         functools.partial(halve_body, lanes=lanes),
@@ -304,7 +303,7 @@
     )(keep, got, early, scale)
 
     hidden = lax.all_gather(hidden, TENSOR, axis=0, tiled=True)
-    own_out = weight_out[0] + sum(x[:1, :1] for x in (arrived, left_gate, right_up, left_up, right_gate)) * 0
+    own_out = weight_out[0] + (from_left[0, :1, :1] + from_right[0, :1, :1]) * 0
     down = lax.all_gather(own_out, "dp", axis=0)
     sending = kernel_call(
         down_body,

time: 207 us -> 182 us (0.88)
  waiting for transfers between devices: 97.9 us -> 67.8 us
  blocking collectives: 11.6 us -> 14.8 us
    ppermute x6 -> x4, waiting for transfers between devices: 50.9 us -> 20.5 us  [the longest x1 20.5 us: per_device(): from_left = lax.ppermute(own_in, 'dp', right)]
    ppermute x2, starting transfers between devices: 7.96 us -> 16.2 us  [per_device(): got = lax.ppermute(send, 'yh', swap)]
    all_to_all x1, starting transfers between devices: 13.9 us -> 9.9 us  [per_device(): lax.all_to_all(outgoing.reshape(experts, FULL, wire), ('z', 'yl'), 0, 0,...]
    all_gather x1, blocking collectives: 11.6 us -> 14.8 us  [per_device(): hidden = lax.all_gather(hidden, TENSOR, axis=0, tiled=True)]
    squeeze x1 -> x2, local copies, waits for them, and re-layouts: 0.12 us -> 3.31 us  [the longest x1 2.2 us: per_device(): far_up = lax.ppermute(from_right[1], 'dp', left)]
    ppermute x6 -> x4, starting transfers between devices: 17.5 us -> 15.5 us  [the longest x1 7.75 us: per_device(): from_left = lax.ppermute(own_in, 'dp', right)]
  transfers between devices with their start and end apart: 13 -> 11, of which waited for: 10 -> 6; matrix products, arithmetic and copies ran while one was open for 1% -> 4% of each run, Pallas kernels for 3% -> 5%
where the time goes in v2:
time: 182 us; the launch traced here: 180 us
  waiting for transfers between devices  67.8 us (37%)
  starting transfers between devices  57.1 us (31%)
  Pallas kernels  17.5 us (10%)
  between operations  15 us (8%)
  blocking collectives  14.8 us (8%)
  local copies, waits for them, and re-layouts  7.05 us (4%)
    all_to_all x1, waiting for transfers between devices, per_device(): lax.all_to_all(sending.reshape(experts, FULL, wire), ('z', 'yl'), 0, 0, t...  36.1 us
    ppermute x1, waiting for transfers between devices, per_device(): from_left = lax.ppermute(own_in, 'dp', right)  20.5 us
    ppermute x2, starting transfers between devices, per_device(): got = lax.ppermute(send, 'yh', swap)  16.2 us
    all_gather x1, blocking collectives, per_device(): hidden = lax.all_gather(hidden, TENSOR, axis=0, tiled=True)  14.8 us
    all_to_all x1, starting transfers between devices, per_device(): lax.all_to_all(sending.reshape(experts, FULL, wire), ('z', 'yl'), 0, 0, t...  11.6 us
    all_to_all x1, starting transfers between devices, per_device(): lax.all_to_all(outgoing.reshape(experts, FULL, wire), ('z', 'yl'), 0, 0,...  9.9 us
    ppermute x1, starting transfers between devices, per_device(): from_left = lax.ppermute(own_in, 'dp', right)  7.75 us
    ppermute x2, waiting for transfers between devices, per_device(): got = lax.ppermute(send, 'yh', swap)  7.49 us
  transfers between devices with their start and end apart: 11, of which 6 were waited for; matrix products, arithmetic and copies ran while one was open for 4% of the time, Pallas kernels for 5%

profile of v2, /device:TPU:6, one launch (start us, length us, event | category | flops | bytes accessed | tf_op | source)
XLA Modules:
  0.0 180.3 jit_solution(8130166892138594151)
XLA Ops:
  6.5 7.8 %collective-permute-start = (bf16[2,1792,256]{2,1,0:T(8,128)(2,1)}, bf16[2,1792,256]{2,1,0:T(8,128)(2,1)S(1)}, u32[]{:S(2)}, u32[]{:S(2)}) collective-permute-start(bf16[2,1792,256]{2,1,0:T(8,128)(2,1)} %bitcast.17), channel_id=1, source_target_pairs={{0,128},{128,256},{256,384},{384,0},{1,129},{129,257},{257,385},{3... | collective-permute-start | bytes 5505032 | tf_op jit(solution)/shard_map/ppermute | solution.py:238
  14.3 1.9 %collective-permute-start.1 = (bf16[2,1792,256]{2,1,0:T(8,128)(2,1)}, bf16[2,1792,256]{2,1,0:T(8,128)(2,1)}, u32[]{:S(2)}, u32[]{:S(2)}) collective-permute-start(bf16[2,1792,256]{2,1,0:T(8,128)(2,1)} %bitcast.18), channel_id=1, source_target_pairs={{0,384},{128,0},{256,128},{384,256},{1,385},{129,1},{257,129},{385... | collective-permute-start | bytes 5505032 | tf_op jit(solution)/shard_map/ppermute | solution.py:239
  16.2 0.0 copy-start
  16.2 1.0 copy-done
  17.2 0.0 copy-start.1
  17.2 0.7 copy-done.1
  17.9 1.9 %shard_map.55 = bf16[256,2688]{1,0:T(8,128)(2,1)} custom-call(s32[2,128]{1,0:T(2,128)S(1)} %bitcast.16, bf16[128,1792]{1,0:T(8,128)(2,1)S(1)} %copy-done), custom_call_target="tpu_custom_call" | custom-call | flops 234881024 | bytes 4194304 | tf_op jit(solution)/shard_map/pallas_call | solution.py:243
  19.9 9.9 %all-to-all-start = ((bf16[32,8,2688]{2,1,0:T(8,128)(2,1)}), bf16[32,8,2688]{2,1,0:T(8,128)(2,1)S(1)}, u32[]{:S(2)}, u32[]{:S(2)}) async-start(bf16[32,8,2688]{2,1,0:T(8,128)(2,1)} %bitcast.4), calls=%async_computation | async-start | bytes 2752512 | tf_op jit(solution)/shard_map/all_to_all | solution.py:251
  29.8 0.0 all-gather.2.cloned.1.call-start
  29.8 0.1 pad_add_fusion.where_ref
  29.9 0.0 copy-start.3
  29.9 20.5 %collective-permute-done.refs_1_ = bf16[2,1792,256]{2,1,0:T(8,128)(2,1)S(1)} collective-permute-done((bf16[2,1792,256]{2,1,0:T(8,128)(2,1)}, bf16[2,1792,256]{2,1,0:T(8,128)(2,1)S(1)}, u32[]{:S(2)}, u32[]{:S(2)}) %collective-permute-start) | collective-permute-done | bytes 1835040 | tf_op jit(solution)/shard_map/ppermute | solution.py:238
  50.4 0.0 copy-start.4
  50.4 1.1 slice_bitcast_fusion.1
  51.5 3.4 %collective-permute-start.2 = (bf16[1792,256]{1,0:T(8,128)(2,1)}, bf16[1792,256]{1,0:T(8,128)(2,1)}, u32[]{:S(2)}, u32[]{:S(2)}) collective-permute-start(bf16[1792,256]{1,0:T(8,128)(2,1)} %slice_bitcast_fusion.1), channel_id=1, source_target_pairs={{0,128},{128,256},{256,384},{384,0},{1,129},{129,257},{257,385},{3... | collective-permute-start | bytes 2752520 | tf_op jit(solution)/shard_map/ppermute | solution.py:240
  54.9 0.0 collective-permute-done.1.refs_2_
  54.9 2.2 %slice_bitcast_fusion = bf16[1792,256]{1,0:T(8,128)(2,1)} fusion(bf16[2,1792,256]{2,1,0:T(8,128)(2,1)} %collective-permute-done.1.refs_2_), kind=kLoop, calls=%fused_computation | loop fusion | bytes 1835008 | tf_op jit(solution)/shard_map/squeeze | solution.py:241
  57.1 2.4 %collective-permute-start.3 = (bf16[1792,256]{1,0:T(8,128)(2,1)}, bf16[1792,256]{1,0:T(8,128)(2,1)}, u32[]{:S(2)}, u32[]{:S(2)}) collective-permute-start(bf16[1792,256]{1,0:T(8,128)(2,1)} %slice_bitcast_fusion), channel_id=1, source_target_pairs={{0,384},{128,0},{256,128},{384,256},{1,385},{129,1},{257,129},{385... | collective-permute-start | bytes 2752520 | tf_op jit(solution)/shard_map/ppermute | solution.py:241
  59.5 0.0 copy-done.4
  59.5 0.5 slice.18
  60.1 1.3 slice.19
  62.7 0.0 copy-done.3
  62.7 1.0 broadcast_add_fusion
  63.7 0.0 all-gather.2.cloned.1.call-update
  63.8 0.3 all-to-all-done
  64.1 5.0 %shard_map.56 = (bf16[192,1664]{1,0:T(8,128)(2,1)S(1)}, f32[192,1664]{1,0:T(8,128)S(1)}, bf16[384,1792]{1,0:T(8,128)(2,1)S(1)}) custom-call(s32[3]{0:T(128)S(1)} %pad_add_fusion.where_ref, bf16[256,2688]{1,0:T(8,128)(2,1)S(1)} %bitcast.15, bf16[2,1792,256]{2,1,0:T(8,128)(2,1)} %bitcast.19, bf16[2,1792,256]{2,1,0:T(8,128)(2,1)} %copy-done.4, ...), custom_call_target="tpu_custom_call" | custom-call | flops 211392921600 | bytes 12582912 | tf_op jit(solution)/shard_map/pallas_call | solution.py:254
  69.1 1.9 %collective-permute-start.6 = (bf16[192,1664]{1,0:T(8,128)(2,1)S(1)}, bf16[192,1664]{1,0:T(8,128)(2,1)S(1)}, u32[]{:S(2)}, u32[]{:S(2)}) collective-permute-start(bf16[192,1664]{1,0:T(8,128)(2,1)S(1)} %get-tuple-element.22), channel_id=1, source_target_pairs={{0,1},{1,0},{2,3},{3,2},{4,5},{5,4},{6,7},{7,6},{8,9},{9,8},{10,11... | collective-permute-start | bytes 1916936 | tf_op jit(solution)/shard_map/ppermute | solution.py:267
  71.0 2.0 %collective-permute-done.6.got_ref = bf16[192,1664]{1,0:T(8,128)(2,1)S(1)} collective-permute-done((bf16[192,1664]{1,0:T(8,128)(2,1)S(1)}, bf16[192,1664]{1,0:T(8,128)(2,1)S(1)}, u32[]{:S(2)}, u32[]{:S(2)}) %collective-permute-start.6) | collective-permute-done | bytes 639008 | tf_op jit(solution)/shard_map/ppermute | solution.py:267
  73.0 0.3 shard_map.59
  73.3 7.4 %collective-permute-start.7 = (bf16[96,1664]{1,0:T(8,128)(2,1)S(1)}, bf16[96,1664]{1,0:T(8,128)(2,1)S(1)}, u32[]{:S(2)}, u32[]{:S(2)}) collective-permute-start(bf16[96,1664]{1,0:T(8,128)(2,1)S(1)} %get-tuple-element.24), channel_id=1, source_target_pairs={{0,2},{2,0},{1,3},{3,1},{4,6},{6,4},{5,7},{7,5},{8,10},{10,8},{9,1... | collective-permute-start | bytes 958472 | tf_op jit(solution)/shard_map/ppermute | solution.py:275
  80.7 0.0 collective-permute-done.2.wg_ref
  80.8 0.0 collective-permute-done.3.wu_ref
  80.8 2.3 %shard_map.57 = (bf16[192,512]{1,0:T(8,128)(2,1)S(1)}, f32[192,512]{1,0:T(8,128)S(1)}) custom-call(bf16[384,1792]{1,0:T(8,128)(2,1)S(1)} %get-tuple-element.16.rows_ref, bf16[1792,256]{1,0:T(8,128)(2,1)} %collective-permute-done.2.wg_ref, bf16[1792,256]{1,0:T(8,128)(2,1)} %collective-permute-done.3.wu_ref), custom_call_target="tpu_custom_call" | custom-call | flops 704643072 | bytes 4194304 | tf_op jit(solution)/shard_map/pallas_call | solution.py:284
  83.1 1.9 %collective-permute-start.4 = (bf16[192,512]{1,0:T(8,128)(2,1)S(1)}, bf16[192,512]{1,0:T(8,128)(2,1)S(1)}, u32[]{:S(2)}, u32[]{:S(2)}) collective-permute-start(bf16[192,512]{1,0:T(8,128)(2,1)S(1)} %get-tuple-element.18), channel_id=1, source_target_pairs={{0,1},{1,0},{2,3},{3,2},{4,5},{5,4},{6,7},{7,6},{8,9},{9,8},{10,11... | collective-permute-start | bytes 589832 | tf_op jit(solution)/shard_map/ppermute | solution.py:292
  85.0 1.4 collective-permute-done.4.got_ref
  86.5 8.8 %collective-permute-start.5 = (bf16[96,512]{1,0:T(8,128)(2,1)S(1)}, bf16[96,512]{1,0:T(8,128)(2,1)S(1)}, u32[]{:S(2)}, u32[]{:S(2)}) collective-permute-start(bf16[96,512]{1,0:T(8,128)(2,1)S(1)} %get-tuple-element.20), channel_id=1, source_target_pairs={{0,2},{2,0},{1,3},{3,1},{4,6},{6,4},{5,7},{7,5},{8,10},{10,8},{9,1... | collective-permute-start | bytes 294920 | tf_op jit(solution)/shard_map/ppermute | solution.py:300
  95.3 0.0 collective-permute-done.7.got_ref
  95.3 0.2 shard_map.60
  95.5 7.5 %collective-permute-done.5.got_ref = bf16[96,512]{1,0:T(8,128)(2,1)S(1)} collective-permute-done((bf16[96,512]{1,0:T(8,128)(2,1)S(1)}, bf16[96,512]{1,0:T(8,128)(2,1)S(1)}, u32[]{:S(2)}, u32[]{:S(2)}) %collective-permute-start.5) | collective-permute-done | bytes 98336 | tf_op jit(solution)/shard_map/ppermute | solution.py:300
  103.0 0.1 shard_map.61
  103.1 14.8 %all_gather.7.hid_ref = bf16[384,1024]{1,0:T(8,128)(2,1)S(1)} all-gather(bf16[96,1024]{1,0:T(8,128)(2,1)S(1)} %shard_map.61), channel_id=1, replica_groups=mesh['dp'=4,'z'=8,'yl'=4,'yh'=2,'core'=2] {'yh','core'}, dimensions={0}, use_global_device_ids=true | all-gather | bytes 983040 | tf_op jit(solution)/shard_map/all_gather | solution.py:305
  117.9 0.0 all-gather.2.cloned.1.call-done.w_ref
  117.9 5.9 %shard_map.62 = bf16[256,2688]{1,0:T(8,128)(2,1)} custom-call(s32[3]{0:T(128)S(1)} %pad_add_fusion.where_ref, bf16[384,1024]{1,0:T(8,128)(2,1)S(1)} %all_gather.7.hid_ref, bf16[4,256,1792]{2,1,0:T(8,128)(2,1)} %all-gather.2.cloned.1.call-done.w_ref), custom_call_target="tpu_custom_call" | custom-call | flops 1879048192 | bytes 6291456 | tf_op jit(solution)/shard_map/pallas_call | solution.py:308
  123.9 0.0 copy-start.2
  123.9 0.0 copy-start.5
  123.9 11.6 %all-to-all-start.1 = ((bf16[32,8,2688]{2,1,0:T(8,128)(2,1)}), bf16[32,8,2688]{2,1,0:T(8,128)(2,1)S(1)}, u32[]{:S(2)}, u32[]{:S(2)}) async-start(bf16[32,8,2688]{2,1,0:T(8,128)(2,1)} %bitcast.10), calls=%async_computation.1 | async-start | bytes 2752512 | tf_op jit(solution)/shard_map/all_to_all | solution.py:322
  135.5 0.0 copy-done.2
  135.5 0.1 copy.8.ids_ref
  135.6 0.0 copy-done.5
  135.6 0.1 copy.9.score_ref
  135.8 36.1 %all-to-all-done.1 = bf16[32,8,2688]{2,1,0:T(8,128)(2,1)S(1)} async-done(((bf16[32,8,2688]{2,1,0:T(8,128)(2,1)}), bf16[32,8,2688]{2,1,0:T(8,128)(2,1)S(1)}, u32[]{:S(2)}, u32[]{:S(2)}) %all-to-all-start.1) | async-done | bytes 1376288 | tf_op jit(solution)/shard_map/all_to_all | solution.py:322
  171.8 1.6 shard_map.63
  (1 shorter events, 0.0 us)
Async XLA Ops:
  6.5 43.8 %collective-permute-start = (bf16[2,1792,256]{2,1,0:T(8,128)(2,1)}, bf16[2,1792,256]{2,1,0:T(8,128)(2,1)S(1)}, u32[]{:S(2)}, u32[]{:S(2)}) collective-permute-start(bf16[2,1792,256]{2,1,0:T(8,128)(2,1)} %bitcast.17), channel_id=1, source_target_pairs={{0,128},{128,256},{256,384},{384,0},{1,129},{129,257},{257,385},{3... | collective-permute-start | bytes 5505032 | tf_op jit(solution)/shard_map/ppermute | solution.py:238
  14.3 40.6 %collective-permute-start.1 = (bf16[2,1792,256]{2,1,0:T(8,128)(2,1)}, bf16[2,1792,256]{2,1,0:T(8,128)(2,1)}, u32[]{:S(2)}, u32[]{:S(2)}) collective-permute-start(bf16[2,1792,256]{2,1,0:T(8,128)(2,1)} %bitcast.18), channel_id=1, source_target_pairs={{0,384},{128,0},{256,128},{384,256},{1,385},{129,1},{257,129},{385... | collective-permute-start | bytes 5505032 | tf_op jit(solution)/shard_map/ppermute | solution.py:239
  16.2 1.0 copy-start
  17.2 0.7 copy-start.1
  19.9 44.2 %all-to-all-start = ((bf16[32,8,2688]{2,1,0:T(8,128)(2,1)}), bf16[32,8,2688]{2,1,0:T(8,128)(2,1)S(1)}, u32[]{:S(2)}, u32[]{:S(2)}) async-start(bf16[32,8,2688]{2,1,0:T(8,128)(2,1)} %bitcast.4), calls=%async_computation | async-start | bytes 2752512 | tf_op jit(solution)/shard_map/all_to_all | solution.py:251
  29.8 88.1 %all-gather.2.cloned.1.call-start = ((), (), s32[]{:S(2)}) async-start(), calls=%async_computation.2 | async-start | bytes 4587520 | tf_op jit(solution)/shard_map/all_gather | solution.py:307
  29.9 32.8 %copy-start.3 = (bf16[1,256,1792]{2,1,0:T(8,128)(2,1)S(1)}, bf16[1,256,1792]{2,1,0:T(8,128)(2,1)}, u32[]{:S(2)}) copy-start(bf16[1,256,1792]{2,1,0:T(8,128)(2,1)} %param.9) | copy-start | bytes 2752516
  50.4 9.2 %copy-start.4 = (bf16[2,1792,256]{2,1,0:T(8,128)(2,1)}, bf16[2,1792,256]{2,1,0:T(8,128)(2,1)S(1)}, u32[]{:S(2)}) copy-start(bf16[2,1792,256]{2,1,0:T(8,128)(2,1)S(1)} %collective-permute-done.refs_1_) | copy-start | bytes 5505028
  51.5 29.3 %collective-permute-start.2 = (bf16[1792,256]{1,0:T(8,128)(2,1)}, bf16[1792,256]{1,0:T(8,128)(2,1)}, u32[]{:S(2)}, u32[]{:S(2)}) collective-permute-start(bf16[1792,256]{1,0:T(8,128)(2,1)} %slice_bitcast_fusion.1), channel_id=1, source_target_pairs={{0,128},{128,256},{256,384},{384,0},{1,129},{129,257},{257,385},{3... | collective-permute-start | bytes 2752520 | tf_op jit(solution)/shard_map/ppermute | solution.py:240
  57.1 23.6 %collective-permute-start.3 = (bf16[1792,256]{1,0:T(8,128)(2,1)}, bf16[1792,256]{1,0:T(8,128)(2,1)}, u32[]{:S(2)}, u32[]{:S(2)}) collective-permute-start(bf16[1792,256]{1,0:T(8,128)(2,1)} %slice_bitcast_fusion), channel_id=1, source_target_pairs={{0,384},{128,0},{256,128},{384,256},{1,385},{129,1},{257,129},{385... | collective-permute-start | bytes 2752520 | tf_op jit(solution)/shard_map/ppermute | solution.py:241
  69.1 4.0 %collective-permute-start.6 = (bf16[192,1664]{1,0:T(8,128)(2,1)S(1)}, bf16[192,1664]{1,0:T(8,128)(2,1)S(1)}, u32[]{:S(2)}, u32[]{:S(2)}) collective-permute-start(bf16[192,1664]{1,0:T(8,128)(2,1)S(1)} %get-tuple-element.22), channel_id=1, source_target_pairs={{0,1},{1,0},{2,3},{3,2},{4,5},{5,4},{6,7},{7,6},{8,9},{9,8},{10,11... | collective-permute-start | bytes 1916936 | tf_op jit(solution)/shard_map/ppermute | solution.py:267
  73.3 22.0 %collective-permute-start.7 = (bf16[96,1664]{1,0:T(8,128)(2,1)S(1)}, bf16[96,1664]{1,0:T(8,128)(2,1)S(1)}, u32[]{:S(2)}, u32[]{:S(2)}) collective-permute-start(bf16[96,1664]{1,0:T(8,128)(2,1)S(1)} %get-tuple-element.24), channel_id=1, source_target_pairs={{0,2},{2,0},{1,3},{3,1},{4,6},{6,4},{5,7},{7,5},{8,10},{10,8},{9,1... | collective-permute-start | bytes 958472 | tf_op jit(solution)/shard_map/ppermute | solution.py:275
  83.1 3.3 %collective-permute-start.4 = (bf16[192,512]{1,0:T(8,128)(2,1)S(1)}, bf16[192,512]{1,0:T(8,128)(2,1)S(1)}, u32[]{:S(2)}, u32[]{:S(2)}) collective-permute-start(bf16[192,512]{1,0:T(8,128)(2,1)S(1)} %get-tuple-element.18), channel_id=1, source_target_pairs={{0,1},{1,0},{2,3},{3,2},{4,5},{5,4},{6,7},{7,6},{8,9},{9,8},{10,11... | collective-permute-start | bytes 589832 | tf_op jit(solution)/shard_map/ppermute | solution.py:292
  86.5 16.5 %collective-permute-start.5 = (bf16[96,512]{1,0:T(8,128)(2,1)S(1)}, bf16[96,512]{1,0:T(8,128)(2,1)S(1)}, u32[]{:S(2)}, u32[]{:S(2)}) collective-permute-start(bf16[96,512]{1,0:T(8,128)(2,1)S(1)} %get-tuple-element.20), channel_id=1, source_target_pairs={{0,2},{2,0},{1,3},{3,1},{4,6},{6,4},{5,7},{7,5},{8,10},{10,8},{9,1... | collective-permute-start | bytes 294920 | tf_op jit(solution)/shard_map/ppermute | solution.py:300
  123.9 11.6 %copy-start.2 = (s32[128,2]{0,1:T(2,128)S(1)}, s32[128,2]{0,1:T(2,128)}, u32[]{:S(2)}) copy-start(s32[128,2]{0,1:T(2,128)} %param.6) | copy-start | bytes 3076
  123.9 11.7 %copy-start.5 = (bf16[128,2]{0,1:T(2,128)(2,1)S(1)}, bf16[128,2]{0,1:T(2,128)(2,1)}, u32[]{:S(2)}) copy-start(bf16[128,2]{0,1:T(2,128)(2,1)} %param.7) | copy-start | bytes 1540
  123.9 47.9 %all-to-all-start.1 = ((bf16[32,8,2688]{2,1,0:T(8,128)(2,1)}), bf16[32,8,2688]{2,1,0:T(8,128)(2,1)S(1)}, u32[]{:S(2)}, u32[]{:S(2)}) async-start(bf16[32,8,2688]{2,1,0:T(8,128)(2,1)} %bitcast.10), calls=%async_computation.1 | async-start | bytes 2752512 | tf_op jit(solution)/shard_map/all_to_all | solution.py:322
Sparse Core Ops, SparseCore 0:
  63.9 51.9 all-gather.1

commit v3 on v2

--- a/solution.py
+++ b/solution.py
@@ -191,14 +191,13 @@
     hid_ref[:, 3 * cols :] = silu_times(both[:, :cols], both[:, cols:]).astype(BF)
 
 
-def down_body(where_ref, hid_ref, w_ref, out_ref, ha, hb, wbuf, sems):
-    chunks, cols, width = w_ref.shape
+def down_body(hid_ref, *refs):
+    weights, (out_ref, ha, hb, wbuf, sems) = refs[:4], refs[4:]
+    cols, width = weights[0].shape
     half = width // 2
-    me = where_ref[2]
-    copies = []
-    for i, step in enumerate((0, 3, 1, 2)):
-        source = lax.rem(me + step, 4)
-        copies.append(pltpu.make_async_copy(w_ref.at[source], wbuf.at[pl.ds(i * cols, cols)], sems.at[i]))
+    copies = [
+        pltpu.make_async_copy(w, wbuf.at[pl.ds(i * cols, cols)], sems.at[i]) for i, w in enumerate(weights)
+    ]
     for copy in copies:
         copy.start()
     quarter = hid_ref.shape[0] // 4
@@ -215,6 +214,16 @@
     out_ref[:, width:] = folded.astype(BF)
 
 
+def half_of(pair, which):
+    def body(pair_ref, out_ref, sem):
+        copy = pltpu.make_async_copy(pair_ref.at[which], out_ref, sem)
+        copy.start()
+        copy.wait()
+
+    out = shape(*pair.shape[1:])
+    return kernel_call(body, out, [HBM], HBM, (pltpu.SemaphoreType.DMA,), flops=3 * 10**10, moved=4 << 20)(in_hbm(pair))
+
+
 def shape(*dims, dtype=BF):
     return jax.ShapeDtypeStruct(dims, dtype)
 
@@ -231,21 +240,22 @@
     first_cols = 6 * cols + lanes
     right = [(i, (i + 1) % 4) for i in range(4)]
     left = [(i, (i - 1) % 4) for i in range(4)]
+    opposite = [(i, (i + 2) % 4) for i in range(4)]
     swap = [(0, 1), (1, 0)]
-    where = jnp.stack([lax.axis_index("core"), lax.axis_index("yh"), lax.axis_index("dp")]).astype(jnp.int32)
+    where = jnp.stack([lax.axis_index("core"), lax.axis_index("yh")]).astype(jnp.int32)
 
     own_in = weight_in[0]
     from_left = lax.ppermute(own_in, "dp", right)
     from_right = lax.ppermute(own_in, "dp", left)
-    far_gate = lax.ppermute(from_left[0], "dp", right)
-    far_up = lax.ppermute(from_right[1], "dp", left)
+    far_gate = lax.ppermute(half_of(from_left, 0), "dp", right)
+    far_up = lax.ppermute(half_of(from_right, 1), "dp", left)
 
     outgoing = kernel_call(
         functools.partial(pack_body, experts=experts),
         shape(experts * FULL, wire),
         [VM, VM],
         VM,
-        flops=1 * 4 * experts * FULL * count * width,
+        flops=4 * experts * FULL * count * width,
         moved=4 << 20,
     )(expert_ids.T, tokens)
     arrived = lax.all_to_all(outgoing.reshape(experts, FULL, wire), ("z", "yl"), 0, 0, tiled=True)
@@ -261,7 +271,7 @@
             pltpu.VMEM((6, width, cols), BF),
             pltpu.SemaphoreType.DMA((3,)),
         ),
-        flops=100 * 12 * slots * width * cols,
+        flops=10 * 12 * slots * width * cols,
         moved=12 << 20,
     )(where, arrived, *map(in_hbm, (own_in, from_left, from_right)))
     got = lax.ppermute(send, "core", swap)
@@ -303,12 +313,12 @@
     )(keep, got, early, scale)
 
     hidden = lax.all_gather(hidden, TENSOR, axis=0, tiled=True)
-    own_out = weight_out[0] + (from_left[0, :1, :1] + from_right[0, :1, :1]) * 0
-    down = lax.all_gather(own_out, "dp", axis=0)
+    own_out = weight_out[0]
+    downs = (own_out, *(lax.ppermute(own_out, "dp", shift) for shift in (right, left, opposite)))
     sending = kernel_call(
         down_body,
         shape(experts * FULL, wire),
-        [SM, VM, HBM],
+        [VM] + [HBM] * 4,
         VM,
         (
             pltpu.VMEM((experts * FULL, 4 * cols), BF),
@@ -318,7 +328,7 @@
         ),
         flops=4 * experts * FULL * 4 * cols * width,
         moved=6 << 20,
-    )(where, hidden, in_hbm(down))
+    )(hidden, *map(in_hbm, downs))
     back = lax.all_to_all(sending.reshape(experts, FULL, wire), ("z", "yl"), 0, 0, tiled=True)
     return kernel_call(
         functools.partial(mix_body, experts=experts),

time: 182 us -> 244 us (1.34)
  Pallas kernels: 17.5 us -> 73.2 us
  between operations: 15 us -> 0.28 us
  waiting for transfers between devices: 67.8 us -> 78.2 us
  starting transfers between devices: 57.1 us -> 67.3 us
  blocking collectives: 14.8 us -> 19 us
    pallas_call x1 -> x3, Pallas kernels: 5.94 us -> 63.2 us  [the longest x2 57.8 us: half_of(): kernel_call(body, out, [HBM], HBM, (pltpu.SemaphoreType.DMA,), flops=3 *...]
    ppermute x2 -> x5, waiting for transfers between devices: 0.01 us -> 17.2 us  [the longest x1 17.2 us: per_device(): far_up = lax.ppermute(half_of(from_right, 1), 'dp', left)]
    ppermute x2 -> x5, starting transfers between devices: 5.82 us -> 15.1 us  [the longest x3 9.3 us: per_device(): lax.ppermute(own_out, 'dp', shift)]
    ppermute x2, waiting for transfers between devices: 7.49 us -> 2.92 us  [per_device(): got = lax.ppermute(send, 'yh', swap)]
    all_gather x1, blocking collectives: 14.8 us -> 19 us  [per_device(): hidden = lax.all_gather(hidden, TENSOR, axis=0, tiled=True)]
    unnamed x14 -> x20, local copies, waits for them, and re-layouts: 1.96 us -> 5.33 us
    squeeze x2 -> x0, local copies, waits for them, and re-layouts: 3.31 us -> none  [the longest x1 2.2 us: per_device(): far_up = lax.ppermute(from_right[1], 'dp', left)]
  transfers between devices with their start and end apart: 11 -> 13, of which waited for: 6 -> 5; matrix products, arithmetic and copies ran while one was open for 4% -> 0% of each run, Pallas kernels for 5% -> 27%
where the time goes in v3:
time: 244 us; the launch traced here: 243 us
  waiting for transfers between devices  78.2 us (32%)
  Pallas kernels  73.2 us (30%)
  starting transfers between devices  67.3 us (28%)
  blocking collectives  19 us (8%)
  local copies, waits for them, and re-layouts  5.33 us (2%)
    pallas_call x2, Pallas kernels, half_of(): kernel_call(body, out, [HBM], HBM, (pltpu.SemaphoreType.DMA,), flops=3 *...  57.8 us
    all_to_all x1, waiting for transfers between devices, per_device(): lax.all_to_all(sending.reshape(experts, FULL, wire), ('z', 'yl'), 0, 0, t...  36.1 us
    ppermute x1, waiting for transfers between devices, per_device(): from_left = lax.ppermute(own_in, 'dp', right)  20.6 us
    all_gather x1, blocking collectives, per_device(): hidden = lax.all_gather(hidden, TENSOR, axis=0, tiled=True)  19 us
    ppermute x2, starting transfers between devices, per_device(): got = lax.ppermute(send, 'yh', swap)  18 us
    ppermute x1, waiting for transfers between devices, per_device(): far_up = lax.ppermute(half_of(from_right, 1), 'dp', left)  17.2 us
    all_to_all x1, starting transfers between devices, per_device(): lax.all_to_all(sending.reshape(experts, FULL, wire), ('z', 'yl'), 0, 0, t...  10.7 us
    all_to_all x1, starting transfers between devices, per_device(): lax.all_to_all(outgoing.reshape(experts, FULL, wire), ('z', 'yl'), 0, 0,...  9.9 us
  transfers between devices with their start and end apart: 13, of which 5 were waited for; matrix products, arithmetic and copies ran while one was open for 0% of the time, Pallas kernels for 27%

profile of v3, /device:TPU:6, one launch (start us, length us, event | category | flops | bytes accessed | tf_op | source)
XLA Modules:
  0.0 243.4 jit_solution(9880062488497680556)
XLA Ops:
  0.0 7.8 %collective-permute-start = (bf16[2,1792,256]{2,1,0:T(8,128)(2,1)}, bf16[2,1792,256]{2,1,0:T(8,128)(2,1)S(1)}, u32[]{:S(2)}, u32[]{:S(2)}) collective-permute-start(bf16[2,1792,256]{2,1,0:T(8,128)(2,1)} %bitcast.12), channel_id=1, source_target_pairs={{0,128},{128,256},{256,384},{384,0},{1,129},{129,257},{257,385},{3... | collective-permute-start | bytes 5505032 | tf_op jit(solution)/shard_map/ppermute | solution.py:248
  7.8 1.9 collective-permute-start.1
  9.7 0.0 copy-start
  9.7 1.0 copy-done
  10.7 0.0 copy-start.1
  10.7 0.7 copy-done.1
  11.4 1.9 shard_map.55
  13.2 9.9 %all-to-all-start = ((bf16[32,8,2688]{2,1,0:T(8,128)(2,1)}), bf16[32,8,2688]{2,1,0:T(8,128)(2,1)S(1)}, u32[]{:S(2)}, u32[]{:S(2)}) async-start(bf16[32,8,2688]{2,1,0:T(8,128)(2,1)} %bitcast.3), calls=%async_computation | async-start | bytes 2752512 | tf_op jit(solution)/shard_map/all_to_all | solution.py:261
  23.2 0.1 pad_add_fusion.where_ref
  23.2 20.6 %collective-permute-done.refs_1_.pair_ref = bf16[2,1792,256]{2,1,0:T(8,128)(2,1)S(1)} collective-permute-done((bf16[2,1792,256]{2,1,0:T(8,128)(2,1)}, bf16[2,1792,256]{2,1,0:T(8,128)(2,1)S(1)}, u32[]{:S(2)}, u32[]{:S(2)}) %collective-permute-start) | collective-permute-done | bytes 1835040 | tf_op jit(solution)/shard_map/ppermute | solution.py:248
  43.8 0.0 copy-start.4
  43.8 1.2 copy-done.4
  45.1 28.9 %shard_map.57 = bf16[1792,256]{1,0:T(8,128)(2,1)} custom-call(bf16[2,1792,256]{2,1,0:T(8,128)(2,1)} %copy-done.4), custom_call_target="tpu_custom_call" | custom-call | flops 30000001024 | bytes 4194304 | tf_op jit(solution)/shard_map/pallas_call | solution.py:224
  74.0 3.4 %collective-permute-start.2 = (bf16[1792,256]{1,0:T(8,128)(2,1)}, bf16[1792,256]{1,0:T(8,128)(2,1)S(1)}, u32[]{:S(2)}, u32[]{:S(2)}) collective-permute-start(bf16[1792,256]{1,0:T(8,128)(2,1)} %shard_map.57), channel_id=1, source_target_pairs={{0,128},{128,256},{256,384},{384,0},{1,129},{129,257},{257,385},{3... | collective-permute-start | bytes 2752520 | tf_op jit(solution)/shard_map/ppermute | solution.py:250
  77.4 0.0 collective-permute-done.1.refs_2_.pair_ref
  77.4 28.9 %shard_map.58 = bf16[1792,256]{1,0:T(8,128)(2,1)} custom-call(bf16[2,1792,256]{2,1,0:T(8,128)(2,1)} %collective-permute-done.1.refs_2_.pair_ref), custom_call_target="tpu_custom_call" | custom-call | flops 30000001024 | bytes 4194304 | tf_op jit(solution)/shard_map/pallas_call | solution.py:224
  106.3 2.4 collective-permute-start.3
  108.7 0.0 all-to-all-done
  108.8 0.0 copy-start.5
  108.8 5.0 %shard_map.56 = (bf16[192,1664]{1,0:T(8,128)(2,1)S(1)}, f32[192,1664]{1,0:T(8,128)S(1)}, bf16[384,1792]{1,0:T(8,128)(2,1)S(1)}) custom-call(s32[2]{0:T(128)S(1)} %pad_add_fusion.where_ref, bf16[256,2688]{1,0:T(8,128)(2,1)S(1)} %bitcast.10, bf16[2,1792,256]{2,1,0:T(8,128)(2,1)} %bitcast.14, bf16[2,1792,256]{2,1,0:T(8,128)(2,1)} %copy-done.4, ...), custom_call_target="tpu_custom_call" | custom-call | flops 21139292160 | bytes 12582912 | tf_op jit(solution)/shard_map/pallas_call | solution.py:264
  113.7 1.9 collective-permute-start.6
  115.7 0.0 copy-done.5
  115.7 3.3 %collective-permute-start.10 = (bf16[256,1792]{1,0:T(8,128)(2,1)S(1)}, bf16[256,1792]{1,0:T(8,128)(2,1)S(1)}, u32[]{:S(2)}, u32[]{:S(2)}) collective-permute-start(bf16[256,1792]{1,0:T(8,128)(2,1)S(1)} %bitcast.16), channel_id=1, source_target_pairs={{0,256},{128,384},{256,0},{384,128},{1,257},{129,385},{257,1},{385... | collective-permute-start | bytes 2752520 | tf_op jit(solution)/shard_map/ppermute | solution.py:317
  119.0 4.0 %collective-permute-start.8 = (bf16[256,1792]{1,0:T(8,128)(2,1)S(1)}, bf16[256,1792]{1,0:T(8,128)(2,1)S(1)}, u32[]{:S(2)}, u32[]{:S(2)}) collective-permute-start(bf16[256,1792]{1,0:T(8,128)(2,1)S(1)} %bitcast.17), channel_id=1, source_target_pairs={{0,128},{128,256},{256,384},{384,0},{1,129},{129,257},{257,385},{3... | collective-permute-start | bytes 2752520 | tf_op jit(solution)/shard_map/ppermute | solution.py:317
  123.0 0.0 collective-permute-done.6.got_ref
  123.0 2.0 collective-permute-start.9
  125.0 0.3 shard_map.61
  125.3 0.0 collective-permute-done.2.wg_ref
  125.3 7.9 %collective-permute-start.7 = (bf16[96,1664]{1,0:T(8,128)(2,1)S(1)}, bf16[96,1664]{1,0:T(8,128)(2,1)S(1)}, u32[]{:S(2)}, u32[]{:S(2)}) collective-permute-start(bf16[96,1664]{1,0:T(8,128)(2,1)S(1)} %get-tuple-element.24), channel_id=1, source_target_pairs={{0,2},{2,0},{1,3},{3,1},{4,6},{6,4},{5,7},{7,5},{8,10},{10,8},{9,1... | collective-permute-start | bytes 958472 | tf_op jit(solution)/shard_map/ppermute | solution.py:285
  133.2 17.2 %collective-permute-done.3.wu_ref = bf16[1792,256]{1,0:T(8,128)(2,1)S(1)} collective-permute-done((bf16[1792,256]{1,0:T(8,128)(2,1)}, bf16[1792,256]{1,0:T(8,128)(2,1)S(1)}, u32[]{:S(2)}, u32[]{:S(2)}) %collective-permute-start.3) | collective-permute-done | bytes 917536 | tf_op jit(solution)/shard_map/ppermute | solution.py:251
  150.4 0.9 shard_map.59
  151.3 1.9 collective-permute-start.4
  153.2 1.4 collective-permute-done.4.got_ref
  154.7 10.1 %collective-permute-start.5 = (bf16[96,512]{1,0:T(8,128)(2,1)S(1)}, bf16[96,512]{1,0:T(8,128)(2,1)S(1)}, u32[]{:S(2)}, u32[]{:S(2)}) collective-permute-start(bf16[96,512]{1,0:T(8,128)(2,1)S(1)} %get-tuple-element.20), channel_id=1, source_target_pairs={{0,2},{2,0},{1,3},{3,1},{4,6},{6,4},{5,7},{7,5},{8,10},{10,8},{9,1... | collective-permute-start | bytes 294920 | tf_op jit(solution)/shard_map/ppermute | solution.py:310
  164.8 0.0 collective-permute-done.7.got_ref
  164.8 0.3 shard_map.62
  165.0 2.9 %collective-permute-done.5.got_ref = bf16[96,512]{1,0:T(8,128)(2,1)S(1)} collective-permute-done((bf16[96,512]{1,0:T(8,128)(2,1)S(1)}, bf16[96,512]{1,0:T(8,128)(2,1)S(1)}, u32[]{:S(2)}, u32[]{:S(2)}) %collective-permute-start.5) | collective-permute-done | bytes 98336 | tf_op jit(solution)/shard_map/ppermute | solution.py:310
  167.9 0.1 shard_map.63
  168.1 19.0 %all_gather.3.hid_ref = bf16[384,1024]{1,0:T(8,128)(2,1)S(1)} all-gather(bf16[96,1024]{1,0:T(8,128)(2,1)S(1)} %shard_map.63), channel_id=1, replica_groups=mesh['dp'=4,'z'=8,'yl'=4,'yh'=2,'core'=2] {'yh','core'}, dimensions={0}, use_global_device_ids=true | all-gather | bytes 983040 | tf_op jit(solution)/shard_map/all_gather | solution.py:315
  187.1 0.0 collective-permute-done.10.refs_3_
  187.1 0.0 copy-start.6
  187.1 0.0 collective-permute-done.8.refs_1_
  187.1 0.0 copy-start.7
  187.1 0.0 collective-permute-done.9.refs_2_
  187.1 0.9 copy-done.6
  188.0 0.3 copy-done.7
  188.3 0.0 copy-start.8
  188.3 0.9 copy-done.8
  189.2 5.4 %shard_map.64 = bf16[256,2688]{1,0:T(8,128)(2,1)} custom-call(bf16[384,1024]{1,0:T(8,128)(2,1)S(1)} %all_gather.3.hid_ref, bf16[256,1792]{1,0:T(8,128)(2,1)} %bitcast.15, bf16[256,1792]{1,0:T(8,128)(2,1)} %copy-done.7, bf16[256,1792]{1,0:T(8,128)(2,1)} %copy-done.8, bf16[256,1792]{1,0:T(8,128)(2,1)} %copy-done.6), custom_call_target="tpu_custom_call" | custom-call | flops 1879048192 | bytes 6291456 | tf_op jit(solution)/shard_map/pallas_call | solution.py:318
  194.7 0.0 copy-start.2
  194.7 0.0 copy-start.3
  194.7 10.7 %all-to-all-start.1 = ((bf16[32,8,2688]{2,1,0:T(8,128)(2,1)}), bf16[32,8,2688]{2,1,0:T(8,128)(2,1)S(1)}, u32[]{:S(2)}, u32[]{:S(2)}) async-start(bf16[32,8,2688]{2,1,0:T(8,128)(2,1)} %bitcast.7), calls=%async_computation.1 | async-start | bytes 2752512 | tf_op jit(solution)/shard_map/all_to_all | solution.py:332
  205.4 0.0 copy-done.2
  205.4 0.1 copy.6.ids_ref
  205.5 0.0 copy-done.3
  205.5 0.1 copy.7.score_ref
  205.7 36.1 %all-to-all-done.1 = bf16[32,8,2688]{2,1,0:T(8,128)(2,1)S(1)} async-done(((bf16[32,8,2688]{2,1,0:T(8,128)(2,1)}), bf16[32,8,2688]{2,1,0:T(8,128)(2,1)S(1)}, u32[]{:S(2)}, u32[]{:S(2)}) %all-to-all-start.1) | async-done | bytes 1376288 | tf_op jit(solution)/shard_map/all_to_all | solution.py:332
  241.7 1.7 shard_map.65
  (1 shorter events, 0.0 us)
Async XLA Ops:
  0.0 43.8 %collective-permute-start = (bf16[2,1792,256]{2,1,0:T(8,128)(2,1)}, bf16[2,1792,256]{2,1,0:T(8,128)(2,1)S(1)}, u32[]{:S(2)}, u32[]{:S(2)}) collective-permute-start(bf16[2,1792,256]{2,1,0:T(8,128)(2,1)} %bitcast.12), channel_id=1, source_target_pairs={{0,128},{128,256},{256,384},{384,0},{1,129},{129,257},{257,385},{3... | collective-permute-start | bytes 5505032 | tf_op jit(solution)/shard_map/ppermute | solution.py:248
  7.8 69.6 %collective-permute-start.1 = (bf16[2,1792,256]{2,1,0:T(8,128)(2,1)}, bf16[2,1792,256]{2,1,0:T(8,128)(2,1)}, u32[]{:S(2)}, u32[]{:S(2)}) collective-permute-start(bf16[2,1792,256]{2,1,0:T(8,128)(2,1)} %bitcast.13), channel_id=1, source_target_pairs={{0,384},{128,0},{256,128},{384,256},{1,385},{129,1},{257,129},{385... | collective-permute-start | bytes 5505032 | tf_op jit(solution)/shard_map/ppermute | solution.py:249
  9.7 1.0 copy-start
  10.7 0.7 copy-start.1
  13.2 95.5 %all-to-all-start = ((bf16[32,8,2688]{2,1,0:T(8,128)(2,1)}), bf16[32,8,2688]{2,1,0:T(8,128)(2,1)S(1)}, u32[]{:S(2)}, u32[]{:S(2)}) async-start(bf16[32,8,2688]{2,1,0:T(8,128)(2,1)} %bitcast.3), calls=%async_computation | async-start | bytes 2752512 | tf_op jit(solution)/shard_map/all_to_all | solution.py:261
  43.8 1.2 copy-start.4
  74.0 51.3 %collective-permute-start.2 = (bf16[1792,256]{1,0:T(8,128)(2,1)}, bf16[1792,256]{1,0:T(8,128)(2,1)S(1)}, u32[]{:S(2)}, u32[]{:S(2)}) collective-permute-start(bf16[1792,256]{1,0:T(8,128)(2,1)} %shard_map.57), channel_id=1, source_target_pairs={{0,128},{128,256},{256,384},{384,0},{1,129},{129,257},{257,385},{3... | collective-permute-start | bytes 2752520 | tf_op jit(solution)/shard_map/ppermute | solution.py:250
  106.3 44.1 %collective-permute-start.3 = (bf16[1792,256]{1,0:T(8,128)(2,1)}, bf16[1792,256]{1,0:T(8,128)(2,1)S(1)}, u32[]{:S(2)}, u32[]{:S(2)}) collective-permute-start(bf16[1792,256]{1,0:T(8,128)(2,1)} %shard_map.58), channel_id=1, source_target_pairs={{0,384},{128,0},{256,128},{384,256},{1,385},{129,1},{257,129},{385... | collective-permute-start | bytes 2752520 | tf_op jit(solution)/shard_map/ppermute | solution.py:251
  108.8 6.9 %copy-start.5 = (bf16[1,256,1792]{2,1,0:T(8,128)(2,1)S(1)}, bf16[1,256,1792]{2,1,0:T(8,128)(2,1)}, u32[]{:S(2)}) copy-start(bf16[1,256,1792]{2,1,0:T(8,128)(2,1)} %param.9) | copy-start | bytes 2752516
  113.7 9.3 %collective-permute-start.6 = (bf16[192,1664]{1,0:T(8,128)(2,1)S(1)}, bf16[192,1664]{1,0:T(8,128)(2,1)S(1)}, u32[]{:S(2)}, u32[]{:S(2)}) collective-permute-start(bf16[192,1664]{1,0:T(8,128)(2,1)S(1)} %get-tuple-element.22), channel_id=1, source_target_pairs={{0,1},{1,0},{2,3},{3,2},{4,5},{5,4},{6,7},{7,6},{8,9},{9,8},{10,11... | collective-permute-start | bytes 1916936 | tf_op jit(solution)/shard_map/ppermute | solution.py:277
  115.7 71.4 %collective-permute-start.10 = (bf16[256,1792]{1,0:T(8,128)(2,1)S(1)}, bf16[256,1792]{1,0:T(8,128)(2,1)S(1)}, u32[]{:S(2)}, u32[]{:S(2)}) collective-permute-start(bf16[256,1792]{1,0:T(8,128)(2,1)S(1)} %bitcast.16), channel_id=1, source_target_pairs={{0,256},{128,384},{256,0},{384,128},{1,257},{129,385},{257,1},{385... | collective-permute-start | bytes 2752520 | tf_op jit(solution)/shard_map/ppermute | solution.py:317
  119.0 68.1 %collective-permute-start.8 = (bf16[256,1792]{1,0:T(8,128)(2,1)S(1)}, bf16[256,1792]{1,0:T(8,128)(2,1)S(1)}, u32[]{:S(2)}, u32[]{:S(2)}) collective-permute-start(bf16[256,1792]{1,0:T(8,128)(2,1)S(1)} %bitcast.17), channel_id=1, source_target_pairs={{0,128},{128,256},{256,384},{384,0},{1,129},{129,257},{257,385},{3... | collective-permute-start | bytes 2752520 | tf_op jit(solution)/shard_map/ppermute | solution.py:317
  123.0 64.0 %collective-permute-start.9 = (bf16[256,1792]{1,0:T(8,128)(2,1)S(1)}, bf16[256,1792]{1,0:T(8,128)(2,1)S(1)}, u32[]{:S(2)}, u32[]{:S(2)}) collective-permute-start(bf16[256,1792]{1,0:T(8,128)(2,1)S(1)} %bitcast.18), channel_id=1, source_target_pairs={{0,384},{128,0},{256,128},{384,256},{1,385},{129,1},{257,129},{385... | collective-permute-start | bytes 2752520 | tf_op jit(solution)/shard_map/ppermute | solution.py:317
  125.3 39.5 %collective-permute-start.7 = (bf16[96,1664]{1,0:T(8,128)(2,1)S(1)}, bf16[96,1664]{1,0:T(8,128)(2,1)S(1)}, u32[]{:S(2)}, u32[]{:S(2)}) collective-permute-start(bf16[96,1664]{1,0:T(8,128)(2,1)S(1)} %get-tuple-element.24), channel_id=1, source_target_pairs={{0,2},{2,0},{1,3},{3,1},{4,6},{6,4},{5,7},{7,5},{8,10},{10,8},{9,1... | collective-permute-start | bytes 958472 | tf_op jit(solution)/shard_map/ppermute | solution.py:285
  151.3 3.3 %collective-permute-start.4 = (bf16[192,512]{1,0:T(8,128)(2,1)S(1)}, bf16[192,512]{1,0:T(8,128)(2,1)S(1)}, u32[]{:S(2)}, u32[]{:S(2)}) collective-permute-start(bf16[192,512]{1,0:T(8,128)(2,1)S(1)} %get-tuple-element.18), channel_id=1, source_target_pairs={{0,1},{1,0},{2,3},{3,2},{4,5},{5,4},{6,7},{7,6},{8,9},{9,8},{10,11... | collective-permute-start | bytes 589832 | tf_op jit(solution)/shard_map/ppermute | solution.py:302
  154.7 13.3 %collective-permute-start.5 = (bf16[96,512]{1,0:T(8,128)(2,1)S(1)}, bf16[96,512]{1,0:T(8,128)(2,1)S(1)}, u32[]{:S(2)}, u32[]{:S(2)}) collective-permute-start(bf16[96,512]{1,0:T(8,128)(2,1)S(1)} %get-tuple-element.20), channel_id=1, source_target_pairs={{0,2},{2,0},{1,3},{3,1},{4,6},{6,4},{5,7},{7,5},{8,10},{10,8},{9,1... | collective-permute-start | bytes 294920 | tf_op jit(solution)/shard_map/ppermute | solution.py:310
  187.1 0.9 copy-start.6
  187.1 1.2 copy-start.7
  188.3 0.9 copy-start.8
  194.7 10.7 %copy-start.2 = (s32[128,2]{0,1:T(2,128)S(1)}, s32[128,2]{0,1:T(2,128)}, u32[]{:S(2)}) copy-start(s32[128,2]{0,1:T(2,128)} %param.6) | copy-start | bytes 3076
  194.7 10.9 %copy-start.3 = (bf16[128,2]{0,1:T(2,128)(2,1)S(1)}, bf16[128,2]{0,1:T(2,128)(2,1)}, u32[]{:S(2)}) copy-start(bf16[128,2]{0,1:T(2,128)(2,1)} %param.7) | copy-start | bytes 1540
  194.7 47.0 %all-to-all-start.1 = ((bf16[32,8,2688]{2,1,0:T(8,128)(2,1)}), bf16[32,8,2688]{2,1,0:T(8,128)(2,1)S(1)}, u32[]{:S(2)}, u32[]{:S(2)}) async-start(bf16[32,8,2688]{2,1,0:T(8,128)(2,1)} %bitcast.7), calls=%async_computation.1 | async-start | bytes 2752512 | tf_op jit(solution)/shard_map/all_to_all | solution.py:332

commit v4 on v3

--- a/solution.py
+++ b/solution.py
@@ -215,13 +215,19 @@
 
 
 def half_of(pair, which):
-    def body(pair_ref, out_ref, sem):
-        copy = pltpu.make_async_copy(pair_ref.at[which], out_ref, sem)
-        copy.start()
-        copy.wait()
-
-    out = shape(*pair.shape[1:])
-    return kernel_call(body, out, [HBM], HBM, (pltpu.SemaphoreType.DMA,), flops=3 * 10**10, moved=4 << 20)(in_hbm(pair))
+    def body(pair_ref, out_ref):
+        out_ref[...] = pair_ref[...]
+
+    rows, cols = pair.shape[1:]
+    return pl.pallas_call(
+        body,
+        grid=(4,),
+        out_shape=shape(rows, cols),
+        in_specs=[pl.BlockSpec((None, rows // 4, cols), lambda i: (which, i, 0))],
+        out_specs=pl.BlockSpec((rows // 4, cols), lambda i: (i, 0)),
+        cost_estimate=pl.CostEstimate(flops=3 * 10**10, transcendentals=0, bytes_accessed=4 * rows * cols),
+        interpret=INTERPRET,
+    )(pair)
 
 
 def shape(*dims, dtype=BF):

time: 244 us -> 193 us (0.79)
  Pallas kernels: 73.2 us -> 22.1 us
    pallas_call x2, Pallas kernels: 57.8 us -> 6.67 us  [half_of(): pl.pallas_call(body, grid=(4,), out_shape=shape(rows, cols), in_specs=[pl...]
  transfers between devices with their start and end apart: 13 -> 13, of which waited for: 5 -> 5; matrix products, arithmetic and copies ran while one was open for 0% -> 0% of each run, Pallas kernels for 27% -> 8%
where the time goes in v4:
time: 193 us; the launch traced here: 192 us
  waiting for transfers between devices  78.2 us (41%)
  starting transfers between devices  67.3 us (35%)
  Pallas kernels  22.1 us (11%)
  blocking collectives  19 us (10%)
  local copies, waits for them, and re-layouts  5.33 us (3%)
    all_to_all x1, waiting for transfers between devices, per_device(): lax.all_to_all(sending.reshape(experts, FULL, wire), ('z', 'yl'), 0, 0, t...  36.1 us
    ppermute x1, waiting for transfers between devices, per_device(): from_left = lax.ppermute(own_in, 'dp', right)  20.6 us
    all_gather x1, blocking collectives, per_device(): hidden = lax.all_gather(hidden, TENSOR, axis=0, tiled=True)  19 us
    ppermute x2, starting transfers between devices, per_device(): got = lax.ppermute(send, 'yh', swap)  18 us
    ppermute x1, waiting for transfers between devices, per_device(): far_up = lax.ppermute(half_of(from_right, 1), 'dp', left)  17.2 us
    all_to_all x1, starting transfers between devices, per_device(): lax.all_to_all(sending.reshape(experts, FULL, wire), ('z', 'yl'), 0, 0, t...  10.7 us
    all_to_all x1, starting transfers between devices, per_device(): lax.all_to_all(outgoing.reshape(experts, FULL, wire), ('z', 'yl'), 0, 0,...  9.9 us
    ppermute x3, starting transfers between devices, per_device(): lax.ppermute(own_out, 'dp', shift)  9.3 us
  transfers between devices with their start and end apart: 13, of which 5 were waited for; matrix products, arithmetic and copies ran while one was open for 0% of the time, Pallas kernels for 8%

profile of v4, /device:TPU:6, one launch (start us, length us, event | category | flops | bytes accessed | tf_op | source)
XLA Modules:
  0.0 192.2 jit_solution(17300287036351757762)
XLA Ops:
  0.0 7.8 %collective-permute-start = (bf16[2,1792,256]{2,1,0:T(8,128)(2,1)}, bf16[2,1792,256]{2,1,0:T(8,128)(2,1)S(1)}, u32[]{:S(2)}, u32[]{:S(2)}) collective-permute-start(bf16[2,1792,256]{2,1,0:T(8,128)(2,1)} %bitcast.12), channel_id=1, source_target_pairs={{0,128},{128,256},{256,384},{384,0},{1,129},{129,257},{257,385},{3... | collective-permute-start | bytes 5505032 | tf_op jit(solution)/shard_map/ppermute | solution.py:254
  7.8 1.9 %collective-permute-start.1 = (bf16[2,1792,256]{2,1,0:T(8,128)(2,1)}, bf16[2,1792,256]{2,1,0:T(8,128)(2,1)}, u32[]{:S(2)}, u32[]{:S(2)}) collective-permute-start(bf16[2,1792,256]{2,1,0:T(8,128)(2,1)} %bitcast.13), channel_id=1, source_target_pairs={{0,384},{128,0},{256,128},{384,256},{1,385},{129,1},{257,129},{385... | collective-permute-start | bytes 5505032 | tf_op jit(solution)/shard_map/ppermute | solution.py:255
  9.7 0.0 copy-start
  9.7 1.0 copy-done
  10.7 0.0 copy-start.1
  10.7 0.7 copy-done.1
  11.4 1.9 shard_map.55
  13.2 9.9 %all-to-all-start = ((bf16[32,8,2688]{2,1,0:T(8,128)(2,1)}), bf16[32,8,2688]{2,1,0:T(8,128)(2,1)S(1)}, u32[]{:S(2)}, u32[]{:S(2)}) async-start(bf16[32,8,2688]{2,1,0:T(8,128)(2,1)} %bitcast.3), calls=%async_computation | async-start | bytes 2752512 | tf_op jit(solution)/shard_map/all_to_all | solution.py:267
  23.2 0.1 pad_add_fusion.where_ref
  23.2 20.6 %collective-permute-done.refs_1_.pair_ref = bf16[2,1792,256]{2,1,0:T(8,128)(2,1)S(1)} collective-permute-done((bf16[2,1792,256]{2,1,0:T(8,128)(2,1)}, bf16[2,1792,256]{2,1,0:T(8,128)(2,1)S(1)}, u32[]{:S(2)}, u32[]{:S(2)}) %collective-permute-start) | collective-permute-done | bytes 1835040 | tf_op jit(solution)/shard_map/ppermute | solution.py:254
  43.8 0.0 copy-start.4
  43.8 1.2 copy-done.4
  45.1 3.3 %shard_map.57 = bf16[1792,256]{1,0:T(8,128)(2,1)} custom-call(bf16[2,1792,256]{2,1,0:T(8,128)(2,1)} %copy-done.4), custom_call_target="tpu_custom_call" | custom-call | flops 30000001024 | bytes 1835008 | tf_op jit(solution)/shard_map/pallas_call | solution.py:222
  48.4 3.4 %collective-permute-start.2 = (bf16[1792,256]{1,0:T(8,128)(2,1)}, bf16[1792,256]{1,0:T(8,128)(2,1)S(1)}, u32[]{:S(2)}, u32[]{:S(2)}) collective-permute-start(bf16[1792,256]{1,0:T(8,128)(2,1)} %shard_map.57), channel_id=1, source_target_pairs={{0,128},{128,256},{256,384},{384,0},{1,129},{129,257},{257,385},{3... | collective-permute-start | bytes 2752520 | tf_op jit(solution)/shard_map/ppermute | solution.py:256
  51.8 0.0 collective-permute-done.1.refs_2_.pair_ref
  51.8 3.3 %shard_map.58 = bf16[1792,256]{1,0:T(8,128)(2,1)} custom-call(bf16[2,1792,256]{2,1,0:T(8,128)(2,1)} %collective-permute-done.1.refs_2_.pair_ref), custom_call_target="tpu_custom_call" | custom-call | flops 30000001024 | bytes 1835008 | tf_op jit(solution)/shard_map/pallas_call | solution.py:222
  55.1 2.4 %collective-permute-start.3 = (bf16[1792,256]{1,0:T(8,128)(2,1)}, bf16[1792,256]{1,0:T(8,128)(2,1)S(1)}, u32[]{:S(2)}, u32[]{:S(2)}) collective-permute-start(bf16[1792,256]{1,0:T(8,128)(2,1)} %shard_map.58), channel_id=1, source_target_pairs={{0,384},{128,0},{256,128},{384,256},{1,385},{129,1},{257,129},{385... | collective-permute-start | bytes 2752520 | tf_op jit(solution)/shard_map/ppermute | solution.py:257
  57.6 0.0 all-to-all-done
  57.6 0.0 copy-start.5
  57.6 5.0 %shard_map.56 = (bf16[192,1664]{1,0:T(8,128)(2,1)S(1)}, f32[192,1664]{1,0:T(8,128)S(1)}, bf16[384,1792]{1,0:T(8,128)(2,1)S(1)}) custom-call(s32[2]{0:T(128)S(1)} %pad_add_fusion.where_ref, bf16[256,2688]{1,0:T(8,128)(2,1)S(1)} %bitcast.10, bf16[2,1792,256]{2,1,0:T(8,128)(2,1)} %bitcast.14, bf16[2,1792,256]{2,1,0:T(8,128)(2,1)} %copy-done.4, ...), custom_call_target="tpu_custom_call" | custom-call | flops 21139292160 | bytes 12582912 | tf_op jit(solution)/shard_map/pallas_call | solution.py:270
  62.6 1.9 collective-permute-start.6
  64.5 0.0 copy-done.5
  64.5 3.3 %collective-permute-start.10 = (bf16[256,1792]{1,0:T(8,128)(2,1)S(1)}, bf16[256,1792]{1,0:T(8,128)(2,1)S(1)}, u32[]{:S(2)}, u32[]{:S(2)}) collective-permute-start(bf16[256,1792]{1,0:T(8,128)(2,1)S(1)} %bitcast.16), channel_id=1, source_target_pairs={{0,256},{128,384},{256,0},{384,128},{1,257},{129,385},{257,1},{385... | collective-permute-start | bytes 2752520 | tf_op jit(solution)/shard_map/ppermute | solution.py:323
  67.8 4.0 %collective-permute-start.8 = (bf16[256,1792]{1,0:T(8,128)(2,1)S(1)}, bf16[256,1792]{1,0:T(8,128)(2,1)S(1)}, u32[]{:S(2)}, u32[]{:S(2)}) collective-permute-start(bf16[256,1792]{1,0:T(8,128)(2,1)S(1)} %bitcast.17), channel_id=1, source_target_pairs={{0,128},{128,256},{256,384},{384,0},{1,129},{129,257},{257,385},{3... | collective-permute-start | bytes 2752520 | tf_op jit(solution)/shard_map/ppermute | solution.py:323
  71.8 0.0 collective-permute-done.6.got_ref
  71.8 2.0 %collective-permute-start.9 = (bf16[256,1792]{1,0:T(8,128)(2,1)S(1)}, bf16[256,1792]{1,0:T(8,128)(2,1)S(1)}, u32[]{:S(2)}, u32[]{:S(2)}) collective-permute-start(bf16[256,1792]{1,0:T(8,128)(2,1)S(1)} %bitcast.18), channel_id=1, source_target_pairs={{0,384},{128,0},{256,128},{384,256},{1,385},{129,1},{257,129},{385... | collective-permute-start | bytes 2752520 | tf_op jit(solution)/shard_map/ppermute | solution.py:323
  73.8 0.3 shard_map.61
  74.1 0.0 collective-permute-done.2.wg_ref
  74.1 7.9 %collective-permute-start.7 = (bf16[96,1664]{1,0:T(8,128)(2,1)S(1)}, bf16[96,1664]{1,0:T(8,128)(2,1)S(1)}, u32[]{:S(2)}, u32[]{:S(2)}) collective-permute-start(bf16[96,1664]{1,0:T(8,128)(2,1)S(1)} %get-tuple-element.24), channel_id=1, source_target_pairs={{0,2},{2,0},{1,3},{3,1},{4,6},{6,4},{5,7},{7,5},{8,10},{10,8},{9,1... | collective-permute-start | bytes 958472 | tf_op jit(solution)/shard_map/ppermute | solution.py:291
  82.1 17.2 %collective-permute-done.3.wu_ref = bf16[1792,256]{1,0:T(8,128)(2,1)S(1)} collective-permute-done((bf16[1792,256]{1,0:T(8,128)(2,1)}, bf16[1792,256]{1,0:T(8,128)(2,1)S(1)}, u32[]{:S(2)}, u32[]{:S(2)}) %collective-permute-start.3) | collective-permute-done | bytes 917536 | tf_op jit(solution)/shard_map/ppermute | solution.py:257
  99.2 0.9 shard_map.59
  100.1 1.9 collective-permute-start.4
  102.0 1.4 collective-permute-done.4.got_ref
  103.5 10.1 %collective-permute-start.5 = (bf16[96,512]{1,0:T(8,128)(2,1)S(1)}, bf16[96,512]{1,0:T(8,128)(2,1)S(1)}, u32[]{:S(2)}, u32[]{:S(2)}) collective-permute-start(bf16[96,512]{1,0:T(8,128)(2,1)S(1)} %get-tuple-element.20), channel_id=1, source_target_pairs={{0,2},{2,0},{1,3},{3,1},{4,6},{6,4},{5,7},{7,5},{8,10},{10,8},{9,1... | collective-permute-start | bytes 294920 | tf_op jit(solution)/shard_map/ppermute | solution.py:316
  113.6 0.0 collective-permute-done.7.got_ref
  113.6 0.3 shard_map.62
  113.9 2.9 %collective-permute-done.5.got_ref = bf16[96,512]{1,0:T(8,128)(2,1)S(1)} collective-permute-done((bf16[96,512]{1,0:T(8,128)(2,1)S(1)}, bf16[96,512]{1,0:T(8,128)(2,1)S(1)}, u32[]{:S(2)}, u32[]{:S(2)}) %collective-permute-start.5) | collective-permute-done | bytes 98336 | tf_op jit(solution)/shard_map/ppermute | solution.py:316
  116.8 0.1 shard_map.63
  116.9 19.0 %all_gather.3.hid_ref = bf16[384,1024]{1,0:T(8,128)(2,1)S(1)} all-gather(bf16[96,1024]{1,0:T(8,128)(2,1)S(1)} %shard_map.63), channel_id=1, replica_groups=mesh['dp'=4,'z'=8,'yl'=4,'yh'=2,'core'=2] {'yh','core'}, dimensions={0}, use_global_device_ids=true | all-gather | bytes 983040 | tf_op jit(solution)/shard_map/all_gather | solution.py:321
  135.9 0.0 collective-permute-done.10.refs_3_
  135.9 0.0 copy-start.6
  135.9 0.0 collective-permute-done.8.refs_1_
  135.9 0.0 copy-start.7
  135.9 0.0 collective-permute-done.9.refs_2_
  135.9 0.9 copy-done.6
  136.8 0.3 copy-done.7
  137.1 0.0 copy-start.8
  137.1 0.9 copy-done.8
  138.1 5.4 %shard_map.64 = bf16[256,2688]{1,0:T(8,128)(2,1)} custom-call(bf16[384,1024]{1,0:T(8,128)(2,1)S(1)} %all_gather.3.hid_ref, bf16[256,1792]{1,0:T(8,128)(2,1)} %bitcast.15, bf16[256,1792]{1,0:T(8,128)(2,1)} %copy-done.7, bf16[256,1792]{1,0:T(8,128)(2,1)} %copy-done.8, bf16[256,1792]{1,0:T(8,128)(2,1)} %copy-done.6), custom_call_target="tpu_custom_call" | custom-call | flops 1879048192 | bytes 6291456 | tf_op jit(solution)/shard_map/pallas_call | solution.py:324
  143.5 0.0 copy-start.2
  143.5 0.0 copy-start.3
  143.5 10.7 %all-to-all-start.1 = ((bf16[32,8,2688]{2,1,0:T(8,128)(2,1)}), bf16[32,8,2688]{2,1,0:T(8,128)(2,1)S(1)}, u32[]{:S(2)}, u32[]{:S(2)}) async-start(bf16[32,8,2688]{2,1,0:T(8,128)(2,1)} %bitcast.7), calls=%async_computation.1 | async-start | bytes 2752512 | tf_op jit(solution)/shard_map/all_to_all | solution.py:338
  154.2 0.0 copy-done.2
  154.2 0.1 copy.6.ids_ref
  154.4 0.0 copy-done.3
  154.4 0.1 copy.7.score_ref
  154.5 36.1 %all-to-all-done.1 = bf16[32,8,2688]{2,1,0:T(8,128)(2,1)S(1)} async-done(((bf16[32,8,2688]{2,1,0:T(8,128)(2,1)}), bf16[32,8,2688]{2,1,0:T(8,128)(2,1)S(1)}, u32[]{:S(2)}, u32[]{:S(2)}) %all-to-all-start.1) | async-done | bytes 1376288 | tf_op jit(solution)/shard_map/all_to_all | solution.py:338
  190.6 1.7 shard_map.65
  (1 shorter events, 0.0 us)
Async XLA Ops:
  0.0 43.8 %collective-permute-start = (bf16[2,1792,256]{2,1,0:T(8,128)(2,1)}, bf16[2,1792,256]{2,1,0:T(8,128)(2,1)S(1)}, u32[]{:S(2)}, u32[]{:S(2)}) collective-permute-start(bf16[2,1792,256]{2,1,0:T(8,128)(2,1)} %bitcast.12), channel_id=1, source_target_pairs={{0,128},{128,256},{256,384},{384,0},{1,129},{129,257},{257,385},{3... | collective-permute-start | bytes 5505032 | tf_op jit(solution)/shard_map/ppermute | solution.py:254
  7.8 44.1 %collective-permute-start.1 = (bf16[2,1792,256]{2,1,0:T(8,128)(2,1)}, bf16[2,1792,256]{2,1,0:T(8,128)(2,1)}, u32[]{:S(2)}, u32[]{:S(2)}) collective-permute-start(bf16[2,1792,256]{2,1,0:T(8,128)(2,1)} %bitcast.13), channel_id=1, source_target_pairs={{0,384},{128,0},{256,128},{384,256},{1,385},{129,1},{257,129},{385... | collective-permute-start | bytes 5505032 | tf_op jit(solution)/shard_map/ppermute | solution.py:255
  9.7 1.0 copy-start
  10.7 0.7 copy-start.1
  13.2 44.3 %all-to-all-start = ((bf16[32,8,2688]{2,1,0:T(8,128)(2,1)}), bf16[32,8,2688]{2,1,0:T(8,128)(2,1)S(1)}, u32[]{:S(2)}, u32[]{:S(2)}) async-start(bf16[32,8,2688]{2,1,0:T(8,128)(2,1)} %bitcast.3), calls=%async_computation | async-start | bytes 2752512 | tf_op jit(solution)/shard_map/all_to_all | solution.py:267
  43.8 1.2 copy-start.4
  48.4 25.7 %collective-permute-start.2 = (bf16[1792,256]{1,0:T(8,128)(2,1)}, bf16[1792,256]{1,0:T(8,128)(2,1)S(1)}, u32[]{:S(2)}, u32[]{:S(2)}) collective-permute-start(bf16[1792,256]{1,0:T(8,128)(2,1)} %shard_map.57), channel_id=1, source_target_pairs={{0,128},{128,256},{256,384},{384,0},{1,129},{129,257},{257,385},{3... | collective-permute-start | bytes 2752520 | tf_op jit(solution)/shard_map/ppermute | solution.py:256
  55.1 44.1 %collective-permute-start.3 = (bf16[1792,256]{1,0:T(8,128)(2,1)}, bf16[1792,256]{1,0:T(8,128)(2,1)S(1)}, u32[]{:S(2)}, u32[]{:S(2)}) collective-permute-start(bf16[1792,256]{1,0:T(8,128)(2,1)} %shard_map.58), channel_id=1, source_target_pairs={{0,384},{128,0},{256,128},{384,256},{1,385},{129,1},{257,129},{385... | collective-permute-start | bytes 2752520 | tf_op jit(solution)/shard_map/ppermute | solution.py:257
  57.6 6.9 %copy-start.5 = (bf16[1,256,1792]{2,1,0:T(8,128)(2,1)S(1)}, bf16[1,256,1792]{2,1,0:T(8,128)(2,1)}, u32[]{:S(2)}) copy-start(bf16[1,256,1792]{2,1,0:T(8,128)(2,1)} %param.9) | copy-start | bytes 2752516
  62.6 9.3 %collective-permute-start.6 = (bf16[192,1664]{1,0:T(8,128)(2,1)S(1)}, bf16[192,1664]{1,0:T(8,128)(2,1)S(1)}, u32[]{:S(2)}, u32[]{:S(2)}) collective-permute-start(bf16[192,1664]{1,0:T(8,128)(2,1)S(1)} %get-tuple-element.22), channel_id=1, source_target_pairs={{0,1},{1,0},{2,3},{3,2},{4,5},{5,4},{6,7},{7,6},{8,9},{9,8},{10,11... | collective-permute-start | bytes 1916936 | tf_op jit(solution)/shard_map/ppermute | solution.py:283
  64.5 71.4 %collective-permute-start.10 = (bf16[256,1792]{1,0:T(8,128)(2,1)S(1)}, bf16[256,1792]{1,0:T(8,128)(2,1)S(1)}, u32[]{:S(2)}, u32[]{:S(2)}) collective-permute-start(bf16[256,1792]{1,0:T(8,128)(2,1)S(1)} %bitcast.16), channel_id=1, source_target_pairs={{0,256},{128,384},{256,0},{384,128},{1,257},{129,385},{257,1},{385... | collective-permute-start | bytes 2752520 | tf_op jit(solution)/shard_map/ppermute | solution.py:323
  67.8 68.1 %collective-permute-start.8 = (bf16[256,1792]{1,0:T(8,128)(2,1)S(1)}, bf16[256,1792]{1,0:T(8,128)(2,1)S(1)}, u32[]{:S(2)}, u32[]{:S(2)}) collective-permute-start(bf16[256,1792]{1,0:T(8,128)(2,1)S(1)} %bitcast.17), channel_id=1, source_target_pairs={{0,128},{128,256},{256,384},{384,0},{1,129},{129,257},{257,385},{3... | collective-permute-start | bytes 2752520 | tf_op jit(solution)/shard_map/ppermute | solution.py:323
  71.8 64.0 %collective-permute-start.9 = (bf16[256,1792]{1,0:T(8,128)(2,1)S(1)}, bf16[256,1792]{1,0:T(8,128)(2,1)S(1)}, u32[]{:S(2)}, u32[]{:S(2)}) collective-permute-start(bf16[256,1792]{1,0:T(8,128)(2,1)S(1)} %bitcast.18), channel_id=1, source_target_pairs={{0,384},{128,0},{256,128},{384,256},{1,385},{129,1},{257,129},{385... | collective-permute-start | bytes 2752520 | tf_op jit(solution)/shard_map/ppermute | solution.py:323
  74.1 39.5 %collective-permute-start.7 = (bf16[96,1664]{1,0:T(8,128)(2,1)S(1)}, bf16[96,1664]{1,0:T(8,128)(2,1)S(1)}, u32[]{:S(2)}, u32[]{:S(2)}) collective-permute-start(bf16[96,1664]{1,0:T(8,128)(2,1)S(1)} %get-tuple-element.24), channel_id=1, source_target_pairs={{0,2},{2,0},{1,3},{3,1},{4,6},{6,4},{5,7},{7,5},{8,10},{10,8},{9,1... | collective-permute-start | bytes 958472 | tf_op jit(solution)/shard_map/ppermute | solution.py:291
  100.1 3.3 %collective-permute-start.4 = (bf16[192,512]{1,0:T(8,128)(2,1)S(1)}, bf16[192,512]{1,0:T(8,128)(2,1)S(1)}, u32[]{:S(2)}, u32[]{:S(2)}) collective-permute-start(bf16[192,512]{1,0:T(8,128)(2,1)S(1)} %get-tuple-element.18), channel_id=1, source_target_pairs={{0,1},{1,0},{2,3},{3,2},{4,5},{5,4},{6,7},{7,6},{8,9},{9,8},{10,11... | collective-permute-start | bytes 589832 | tf_op jit(solution)/shard_map/ppermute | solution.py:308
  103.5 13.3 %collective-permute-start.5 = (bf16[96,512]{1,0:T(8,128)(2,1)S(1)}, bf16[96,512]{1,0:T(8,128)(2,1)S(1)}, u32[]{:S(2)}, u32[]{:S(2)}) collective-permute-start(bf16[96,512]{1,0:T(8,128)(2,1)S(1)} %get-tuple-element.20), channel_id=1, source_target_pairs={{0,2},{2,0},{1,3},{3,1},{4,6},{6,4},{5,7},{7,5},{8,10},{10,8},{9,1... | collective-permute-start | bytes 294920 | tf_op jit(solution)/shard_map/ppermute | solution.py:316
  135.9 0.9 copy-start.6
  135.9 1.2 copy-start.7
  137.1 0.9 copy-start.8
  143.5 10.7 %copy-start.2 = (s32[128,2]{0,1:T(2,128)S(1)}, s32[128,2]{0,1:T(2,128)}, u32[]{:S(2)}) copy-start(s32[128,2]{0,1:T(2,128)} %param.6) | copy-start | bytes 3076
  143.5 10.9 %copy-start.3 = (bf16[128,2]{0,1:T(2,128)(2,1)S(1)}, bf16[128,2]{0,1:T(2,128)(2,1)}, u32[]{:S(2)}) copy-start(bf16[128,2]{0,1:T(2,128)(2,1)} %param.7) | copy-start | bytes 1540
  143.5 47.0 %all-to-all-start.1 = ((bf16[32,8,2688]{2,1,0:T(8,128)(2,1)}), bf16[32,8,2688]{2,1,0:T(8,128)(2,1)S(1)}, u32[]{:S(2)}, u32[]{:S(2)}) async-start(bf16[32,8,2688]{2,1,0:T(8,128)(2,1)} %bitcast.7), calls=%async_computation.1 | async-start | bytes 2752512 | tf_op jit(solution)/shard_map/all_to_all | solution.py:338

commit v5 on v2

--- a/solution.py
+++ b/solution.py
@@ -16,6 +16,7 @@
 VM = pl.BlockSpec(memory_space=pltpu.VMEM)
 SM = pl.BlockSpec(memory_space=pltpu.SMEM)
 HBM = pl.BlockSpec(memory_space=pltpu.HBM)
+ANY = pl.BlockSpec(memory_space=pl.ANY)
 
 
 def kernel_call(body, out_shape, in_specs, out_specs, scratch=(), flops=0, moved=0):
@@ -117,13 +118,14 @@
     fulls, extras = quarter * 2 // 3, quarter // 3
     half = width // 2
     cols = wbuf.shape[2]
-    copies = [pltpu.make_async_copy(w, wbuf.at[pl.ds(2 * i, 2)], sems.at[i]) for i, w in enumerate(weights)]
+    core, yh = where_ref[0], where_ref[1]
+    places = (0, 2 + 2 * core, 4 - 2 * core)
+    copies = [pltpu.make_async_copy(w, wbuf.at[pl.ds(places[i], 2)], sems.at[i]) for i, w in enumerate(weights)]
     for copy in copies:
         copy.start()
     folded = arrived_ref[:, width:]
     extra[:, :half] = dot(fold_rows(4 * extras, 0), folded).astype(BF)
     extra[:, half:] = dot(fold_rows(4 * extras, 1), folded).astype(BF)
-    core, yh = where_ref[0], where_ref[1]
     for q in range(4):
         core_q = 1 - core if q < 2 else core
         yh_q = 1 - yh if q % 2 == 0 else yh
@@ -137,20 +139,23 @@
         squares = jnp.sum(part * part, axis=1, keepdims=True)
         lanes = out_ref.shape[1] - 6 * cols
         out_ref[:, 6 * cols :] = split_in_two(squares, lanes).astype(out_ref.dtype)
-    for i, copy in enumerate(copies):
-        copy.wait()
+    for i in range(3):
+        if i < 2:
+            copies[i].wait()
+        if i == 1:
+            copies[2].wait()
         for at in range(2 * i, 2 * i + 2):
             to = slice(at * cols, (at + 1) * cols)
             send_ref[:, to] = dot(rows_ref[:middle, :], wbuf[at]).astype(BF)
             keep_ref[:, to] = dot(rows_ref[middle:, :], wbuf[at])
 
 
-def last_body(rows_ref, wg_ref, wu_ref, send_ref, keep_ref):
+def last_body(rows_ref, w_ref, send_ref, keep_ref):
     middle = rows_ref.shape[0] // 2
-    cols = wg_ref.shape[1]
-    for g, w in enumerate((wg_ref, wu_ref)):
-        send_ref[:, g * cols : (g + 1) * cols] = dot(rows_ref[:middle, :], w[...]).astype(BF)
-        keep_ref[:, g * cols : (g + 1) * cols] = dot(rows_ref[middle:, :], w[...])
+    cols = w_ref.shape[2]
+    for g in range(2):
+        send_ref[:, g * cols : (g + 1) * cols] = dot(rows_ref[:middle, :], w_ref[g]).astype(BF)
+        keep_ref[:, g * cols : (g + 1) * cols] = dot(rows_ref[middle:, :], w_ref[g])
 
 
 def halve_body(keep_ref, got_ref, send_ref, own_ref, *, lanes):
@@ -219,6 +224,22 @@
     return jax.ShapeDtypeStruct(dims, dtype)
 
 
+def handed_on(x, after):
+    def body(x_ref, *refs):
+        refs[-1][...] = x_ref[...]
+
+    rows, cols = x.shape
+    return pl.pallas_call(
+        body,
+        grid=(2,),
+        out_shape=shape(rows, cols),
+        in_specs=[pl.BlockSpec((rows // 2, cols), lambda i: (i, 0))] + [ANY] * len(after),
+        out_specs=pl.BlockSpec((rows // 2, cols), lambda i: (i, 0)),
+        cost_estimate=pl.CostEstimate(flops=10000000000, transcendentals=0, bytes_accessed=4 * rows * cols),
+        interpret=INTERPRET,
+    )(x, *after)
+
+
 def per_device(tokens, expert_ids, gate_scores, weight_in, weight_out):
     experts = lax.axis_size("z") * lax.axis_size("yl")
     count, width = tokens.shape
@@ -229,16 +250,16 @@
     half, part = slots // 2, slots // 4
     lanes = 128
     first_cols = 6 * cols + lanes
-    right = [(i, (i + 1) % 4) for i in range(4)]
-    left = [(i, (i - 1) % 4) for i in range(4)]
     swap = [(0, 1), (1, 0)]
     where = jnp.stack([lax.axis_index("core"), lax.axis_index("yh"), lax.axis_index("dp")]).astype(jnp.int32)
 
     own_in = weight_in[0]
-    from_left = lax.ppermute(own_in, "dp", right)
-    from_right = lax.ppermute(own_in, "dp", left)
-    far_gate = lax.ppermute(from_left[0], "dp", right)
-    far_up = lax.ppermute(from_right[1], "dp", left)
+    ring = ("dp", "core")
+    forth = [(2 * i + c, 2 * ((i + 1 - 2 * c) % 4) + c) for i in range(4) for c in range(2)]
+    back = [(target, source) for source, target in forth]
+    near_in = lax.ppermute(own_in, ring, forth)
+    other_in = lax.ppermute(own_in, ring, back)
+    far_in = lax.ppermute(near_in, ring, forth)
 
     outgoing = kernel_call(
         functools.partial(pack_body, experts=experts),
@@ -261,9 +282,9 @@
             pltpu.VMEM((6, width, cols), BF),
             pltpu.SemaphoreType.DMA((3,)),
         ),
-        flops=100 * 12 * slots * width * cols,
+        flops=10 * 12 * slots * width * cols,
         moved=12 << 20,
-    )(where, arrived, *map(in_hbm, (own_in, from_left, from_right)))
+    )(where, arrived, *map(in_hbm, (own_in, near_in, other_in)))
     got = lax.ppermute(send, "core", swap)
     send, keep = kernel_call(
         functools.partial(halve_body, lanes=lanes),
@@ -284,11 +305,11 @@
     send, keep = kernel_call(
         last_body,
         (shape(half, 2 * cols), shape(half, 2 * cols, dtype=F32)),
-        [VM, VM, VM],
+        [VM, VM],
         (VM, VM),
         flops=4 * slots * width * cols,
         moved=4 << 20,
-    )(rows, far_gate, far_up)
+    )(rows, far_in)
     got = lax.ppermute(send, "core", swap)
     send, keep = kernel_call(
         functools.partial(halve_body, lanes=0),
@@ -303,7 +324,7 @@
     )(keep, got, early, scale)
 
     hidden = lax.all_gather(hidden, TENSOR, axis=0, tiled=True)
-    own_out = weight_out[0] + (from_left[0, :1, :1] + from_right[0, :1, :1]) * 0
+    own_out = handed_on(weight_out[0], (near_in, other_in))
     down = lax.all_gather(own_out, "dp", axis=0)
     sending = kernel_call(
         down_body,
@@ -319,7 +340,7 @@
         flops=4 * experts * FULL * 4 * cols * width,
         moved=6 << 20,
     )(where, hidden, in_hbm(down))
-    back = lax.all_to_all(sending.reshape(experts, FULL, wire), ("z", "yl"), 0, 0, tiled=True)
+    returned = lax.all_to_all(sending.reshape(experts, FULL, wire), ("z", "yl"), 0, 0, tiled=True)
     return kernel_call(
         functools.partial(mix_body, experts=experts),
         shape(count, width),
@@ -327,7 +348,7 @@
         VM,
         flops=4 * experts * FULL * count * width,
         moved=2 << 20,
-    )(expert_ids, gate_scores, back.reshape(experts * FULL, wire))
+    )(expert_ids, gate_scores, returned.reshape(experts * FULL, wire))
 
 
 def solution(mesh):

time: 182 us -> 194 us (1.066)
  waiting for transfers between devices: 67.8 us -> 97 us
  starting transfers between devices: 57.1 us -> 49.9 us
  local copies, waits for them, and re-layouts: 7.05 us -> 3.21 us
  blocking collectives: 14.8 us -> 11.1 us
    ppermute x4 -> x3, waiting for transfers between devices: 20.5 us -> 40.6 us  [the longest x1 23 us: per_device(): near_in = lax.ppermute(own_in, ring, forth)]
    ppermute x2, starting transfers between devices: 16.2 us -> 7.6 us  [per_device(): got = lax.ppermute(send, 'yh', swap)]
    ppermute x2, waiting for transfers between devices: 7.49 us -> 12.7 us  [per_device(): got = lax.ppermute(send, 'yh', swap)]
    all_to_all x1, waiting for transfers between devices: 0.32 us -> 4.25 us  [per_device(): lax.all_to_all(outgoing.reshape(experts, FULL, wire), ('z', 'yl'), 0, 0,...]
    all_gather x1, blocking collectives: 14.8 us -> 11.1 us  [per_device(): hidden = lax.all_gather(hidden, TENSOR, axis=0, tiled=True)]
    squeeze x2 -> x0, local copies, waits for them, and re-layouts: 3.31 us -> none  [the longest x1 2.2 us: per_device(): far_up = lax.ppermute(from_right[1], 'dp', left)]
    pallas_call x0 -> x1, Pallas kernels: none -> 2.01 us  [handed_on(): pl.pallas_call(body, grid=(2,), out_shape=shape(rows, cols), in_specs=[pl...]
    ppermute x4 -> x3, starting transfers between devices: 15.5 us -> 15.2 us  [the longest x1 7.75 us: per_device(): near_in = lax.ppermute(own_in, ring, forth)]
  transfers between devices with their start and end apart: 11 -> 10, of which waited for: 6 -> 7; matrix products, arithmetic and copies ran while one was open for 4% -> 0% of each run, Pallas kernels for 5% -> 6%
where the time goes in v5:
time: 194 us; the launch traced here: 193 us
  waiting for transfers between devices  97 us (50%)
  starting transfers between devices  49.9 us (26%)
  Pallas kernels  18.2 us (9%)
  between operations  13.6 us (7%)
  blocking collectives  11.1 us (6%)
  local copies, waits for them, and re-layouts  3.21 us (2%)
    all_to_all x1, waiting for transfers between devices, per_device(): lax.all_to_all(sending.reshape(experts, FULL, wire), ('z', 'yl'), 0, 0, t...  36.1 us
    ppermute x1, waiting for transfers between devices, per_device(): near_in = lax.ppermute(own_in, ring, forth)  23 us
    ppermute x1, waiting for transfers between devices, per_device(): far_in = lax.ppermute(near_in, ring, forth)  17.5 us
    all_to_all x1, starting transfers between devices, per_device(): lax.all_to_all(sending.reshape(experts, FULL, wire), ('z', 'yl'), 0, 0, t...  13.3 us
    ppermute x2, waiting for transfers between devices, per_device(): got = lax.ppermute(send, 'yh', swap)  12.7 us
    all_gather x1, blocking collectives, per_device(): hidden = lax.all_gather(hidden, TENSOR, axis=0, tiled=True)  11.1 us
    all_to_all x1, starting transfers between devices, per_device(): lax.all_to_all(outgoing.reshape(experts, FULL, wire), ('z', 'yl'), 0, 0,...  9.9 us
    ppermute x1, starting transfers between devices, per_device(): near_in = lax.ppermute(own_in, ring, forth)  7.75 us
  transfers between devices with their start and end apart: 10, of which 7 were waited for; matrix products, arithmetic and copies ran while one was open for 0% of the time, Pallas kernels for 6%

profile of v5, /device:TPU:6, one launch (start us, length us, event | category | flops | bytes accessed | tf_op | source)
XLA Modules:
  0.0 193.1 jit_solution(4339283514748740382)
XLA Ops:
  6.5 7.8 %collective-permute-start = (bf16[2,1792,256]{2,1,0:T(8,128)(2,1)}, bf16[2,1792,256]{2,1,0:T(8,128)(2,1)S(1)}, u32[]{:S(2)}, u32[]{:S(2)}) collective-permute-start(bf16[2,1792,256]{2,1,0:T(8,128)(2,1)} %bitcast.15), channel_id=1, source_target_pairs={{0,128},{1,385},{128,256},{129,1},{256,384},{257,129},{384,0},{385... | collective-permute-start | bytes 5505032 | tf_op jit(solution)/shard_map/ppermute | solution.py:260
  14.3 1.9 collective-permute-start.1
  16.2 0.0 copy-start
  16.2 1.0 copy-done
  17.2 0.0 copy-start.1
  17.2 0.7 copy-done.1
  17.9 2.0 %shard_map.55 = bf16[256,2688]{1,0:T(8,128)(2,1)} custom-call(s32[2,128]{1,0:T(2,128)S(1)} %bitcast.13, bf16[128,1792]{1,0:T(8,128)(2,1)S(1)} %copy-done), custom_call_target="tpu_custom_call" | custom-call | flops 234881024 | bytes 4194304 | tf_op jit(solution)/shard_map/pallas_call | solution.py:264
  19.9 9.9 %all-to-all-start = ((bf16[32,8,2688]{2,1,0:T(8,128)(2,1)}), bf16[32,8,2688]{2,1,0:T(8,128)(2,1)S(1)}, u32[]{:S(2)}, u32[]{:S(2)}) async-start(bf16[32,8,2688]{2,1,0:T(8,128)(2,1)} %bitcast.4), calls=%async_computation | async-start | bytes 2752512 | tf_op jit(solution)/shard_map/all_to_all | solution.py:272
  29.8 0.0 all-gather.3.cloned.1.call-start
  29.8 23.0 %collective-permute-done.refs_1_.refs_0_ = bf16[2,1792,256]{2,1,0:T(8,128)(2,1)S(1)} collective-permute-done((bf16[2,1792,256]{2,1,0:T(8,128)(2,1)}, bf16[2,1792,256]{2,1,0:T(8,128)(2,1)S(1)}, u32[]{:S(2)}, u32[]{:S(2)}) %collective-permute-start) | collective-permute-done | bytes 1835040 | tf_op jit(solution)/shard_map/ppermute | solution.py:260
  52.9 0.0 copy-start.4
  52.9 0.0 collective-permute-done.1.refs_2_.refs_1_
  52.9 1.3 copy-done.4
  54.1 2.0 %shard_map.62 = bf16[256,1792]{1,0:T(8,128)(2,1)} custom-call(bf16[256,1792]{1,0:T(8,128)(2,1)} %bitcast.18, bf16[2,1792,256]{2,1,0:T(8,128)(2,1)} %copy-done.4, bf16[2,1792,256]{2,1,0:T(8,128)(2,1)} %collective-permute-done.1.refs_2_.refs_1_), custom_call_target="tpu_custom_call" | custom-call | flops 10000000000 | bytes 1835008 | tf_op jit(solution)/shard_map/pallas_call | solution.py:232
  56.2 0.0 all-gather.3.cloned.1.call-update
  56.2 0.1 pad_add_fusion.where_ref
  56.3 5.5 %collective-permute-start.2 = (bf16[2,1792,256]{2,1,0:T(8,128)(2,1)}, bf16[2,1792,256]{2,1,0:T(8,128)(2,1)S(1)}, u32[]{:S(2)}, u32[]{:S(2)}) collective-permute-start(bf16[2,1792,256]{2,1,0:T(8,128)(2,1)} %copy-done.4), channel_id=1, source_target_pairs={{0,128},{1,385},{128,256},{129,1},{256,384},{257,129},{384,0},{385... | collective-permute-start | bytes 5505032 | tf_op jit(solution)/shard_map/ppermute | solution.py:262
  61.8 4.2 %all-to-all-done = bf16[32,8,2688]{2,1,0:T(8,128)(2,1)S(1)} async-done(((bf16[32,8,2688]{2,1,0:T(8,128)(2,1)}), bf16[32,8,2688]{2,1,0:T(8,128)(2,1)S(1)}, u32[]{:S(2)}, u32[]{:S(2)}) %all-to-all-start) | async-done | bytes 1376288 | tf_op jit(solution)/shard_map/all_to_all | solution.py:272
  66.0 5.1 %shard_map.56 = (bf16[192,1664]{1,0:T(8,128)(2,1)S(1)}, f32[192,1664]{1,0:T(8,128)S(1)}, bf16[384,1792]{1,0:T(8,128)(2,1)S(1)}) custom-call(s32[3]{0:T(128)S(1)} %pad_add_fusion.where_ref, bf16[256,2688]{1,0:T(8,128)(2,1)S(1)} %bitcast.12, bf16[2,1792,256]{2,1,0:T(8,128)(2,1)} %bitcast.17, bf16[2,1792,256]{2,1,0:T(8,128)(2,1)} %copy-done.4, ...), custom_call_target="tpu_custom_call" | custom-call | flops 21139292160 | bytes 12582912 | tf_op jit(solution)/shard_map/pallas_call | solution.py:275
  71.2 1.9 collective-permute-start.5
  73.1 2.0 %collective-permute-done.5.got_ref = bf16[192,1664]{1,0:T(8,128)(2,1)S(1)} collective-permute-done((bf16[192,1664]{1,0:T(8,128)(2,1)S(1)}, bf16[192,1664]{1,0:T(8,128)(2,1)S(1)}, u32[]{:S(2)}, u32[]{:S(2)}) %collective-permute-start.5) | collective-permute-done | bytes 639008 | tf_op jit(solution)/shard_map/ppermute | solution.py:288
  75.1 0.3 shard_map.59
  75.4 5.7 %collective-permute-start.6 = (bf16[96,1664]{1,0:T(8,128)(2,1)S(1)}, bf16[96,1664]{1,0:T(8,128)(2,1)S(1)}, u32[]{:S(2)}, u32[]{:S(2)}) collective-permute-start(bf16[96,1664]{1,0:T(8,128)(2,1)S(1)} %get-tuple-element.24), channel_id=1, source_target_pairs={{0,2},{2,0},{1,3},{3,1},{4,6},{6,4},{5,7},{7,5},{8,10},{10,8},{9,1... | collective-permute-start | bytes 958472 | tf_op jit(solution)/shard_map/ppermute | solution.py:296
  81.1 17.5 %collective-permute-done.2.w_ref = bf16[2,1792,256]{2,1,0:T(8,128)(2,1)S(1)} collective-permute-done((bf16[2,1792,256]{2,1,0:T(8,128)(2,1)}, bf16[2,1792,256]{2,1,0:T(8,128)(2,1)S(1)}, u32[]{:S(2)}, u32[]{:S(2)}) %collective-permute-start.2) | collective-permute-done | bytes 1835040 | tf_op jit(solution)/shard_map/ppermute | solution.py:262
  98.6 0.9 shard_map.57
  99.5 1.9 collective-permute-start.3
  101.4 1.4 collective-permute-done.3.got_ref
  102.9 1.9 collective-permute-start.4
  104.8 0.0 collective-permute-done.6.got_ref
  104.8 0.3 shard_map.60
  105.1 12.7 %collective-permute-done.4.got_ref = bf16[96,512]{1,0:T(8,128)(2,1)S(1)} collective-permute-done((bf16[96,512]{1,0:T(8,128)(2,1)S(1)}, bf16[96,512]{1,0:T(8,128)(2,1)S(1)}, u32[]{:S(2)}, u32[]{:S(2)}) %collective-permute-start.4) | collective-permute-done | bytes 98336 | tf_op jit(solution)/shard_map/ppermute | solution.py:321
  117.7 0.1 shard_map.61
  117.9 11.1 %all_gather.9.hid_ref = bf16[384,1024]{1,0:T(8,128)(2,1)S(1)} all-gather(bf16[96,1024]{1,0:T(8,128)(2,1)S(1)} %shard_map.61), channel_id=1, replica_groups=mesh['dp'=4,'z'=8,'yl'=4,'yh'=2,'core'=2] {'yh','core'}, dimensions={0}, use_global_device_ids=true | all-gather | bytes 983040 | tf_op jit(solution)/shard_map/all_gather | solution.py:326
  129.0 0.0 all-gather.3.cloned.1.call-done
  129.0 5.9 %shard_map.63 = bf16[256,2688]{1,0:T(8,128)(2,1)} custom-call(s32[3]{0:T(128)S(1)} %pad_add_fusion.where_ref, bf16[384,1024]{1,0:T(8,128)(2,1)S(1)} %all_gather.9.hid_ref, bf16[4,256,1792]{2,1,0:T(8,128)(2,1)} %bitcast.14), custom_call_target="tpu_custom_call" | custom-call | flops 1879048192 | bytes 6291456 | tf_op jit(solution)/shard_map/pallas_call | solution.py:329
  134.9 0.0 copy-start.2
  135.0 0.0 copy-start.3
  135.0 13.3 %all-to-all-start.1 = ((bf16[32,8,2688]{2,1,0:T(8,128)(2,1)}), bf16[32,8,2688]{2,1,0:T(8,128)(2,1)S(1)}, u32[]{:S(2)}, u32[]{:S(2)}) async-start(bf16[32,8,2688]{2,1,0:T(8,128)(2,1)} %bitcast.9), calls=%async_computation.1 | async-start | bytes 2752512 | tf_op jit(solution)/shard_map/all_to_all | solution.py:343
  148.3 0.0 copy-done.2
  148.3 0.1 copy.6.ids_ref
  148.4 0.0 copy-done.3
  148.4 0.1 copy.7.score_ref
  148.6 36.1 %all-to-all-done.1 = bf16[32,8,2688]{2,1,0:T(8,128)(2,1)S(1)} async-done(((bf16[32,8,2688]{2,1,0:T(8,128)(2,1)}), bf16[32,8,2688]{2,1,0:T(8,128)(2,1)S(1)}, u32[]{:S(2)}, u32[]{:S(2)}) %all-to-all-start.1) | async-done | bytes 1376288 | tf_op jit(solution)/shard_map/all_to_all | solution.py:343
  184.6 1.6 shard_map.64
  (1 shorter events, 0.0 us)
Async XLA Ops:
  6.5 46.3 %collective-permute-start = (bf16[2,1792,256]{2,1,0:T(8,128)(2,1)}, bf16[2,1792,256]{2,1,0:T(8,128)(2,1)S(1)}, u32[]{:S(2)}, u32[]{:S(2)}) collective-permute-start(bf16[2,1792,256]{2,1,0:T(8,128)(2,1)} %bitcast.15), channel_id=1, source_target_pairs={{0,128},{1,385},{128,256},{129,1},{256,384},{257,129},{384,0},{385... | collective-permute-start | bytes 5505032 | tf_op jit(solution)/shard_map/ppermute | solution.py:260
  14.3 38.6 %collective-permute-start.1 = (bf16[2,1792,256]{2,1,0:T(8,128)(2,1)}, bf16[2,1792,256]{2,1,0:T(8,128)(2,1)}, u32[]{:S(2)}, u32[]{:S(2)}) collective-permute-start(bf16[2,1792,256]{2,1,0:T(8,128)(2,1)} %bitcast.16), channel_id=1, source_target_pairs={{128,0},{385,1},{256,128},{1,129},{384,256},{129,257},{0,384},{257... | collective-permute-start | bytes 5505032 | tf_op jit(solution)/shard_map/ppermute | solution.py:261
  16.2 1.0 copy-start
  17.2 0.7 copy-start.1
  19.9 46.1 %all-to-all-start = ((bf16[32,8,2688]{2,1,0:T(8,128)(2,1)}), bf16[32,8,2688]{2,1,0:T(8,128)(2,1)S(1)}, u32[]{:S(2)}, u32[]{:S(2)}) async-start(bf16[32,8,2688]{2,1,0:T(8,128)(2,1)} %bitcast.4), calls=%async_computation | async-start | bytes 2752512 | tf_op jit(solution)/shard_map/all_to_all | solution.py:272
  29.8 99.2 %all-gather.3.cloned.1.call-start = ((), (), s32[]{:S(2)}) async-start(), calls=%async_computation.2 | async-start | bytes 4587520 | tf_op jit(solution)/shard_map/all_gather | solution.py:328
  52.9 1.3 copy-start.4
  56.3 42.4 %collective-permute-start.2 = (bf16[2,1792,256]{2,1,0:T(8,128)(2,1)}, bf16[2,1792,256]{2,1,0:T(8,128)(2,1)S(1)}, u32[]{:S(2)}, u32[]{:S(2)}) collective-permute-start(bf16[2,1792,256]{2,1,0:T(8,128)(2,1)} %copy-done.4), channel_id=1, source_target_pairs={{0,128},{1,385},{128,256},{129,1},{256,384},{257,129},{384,0},{385... | collective-permute-start | bytes 5505032 | tf_op jit(solution)/shard_map/ppermute | solution.py:262
  71.2 4.0 %collective-permute-start.5 = (bf16[192,1664]{1,0:T(8,128)(2,1)S(1)}, bf16[192,1664]{1,0:T(8,128)(2,1)S(1)}, u32[]{:S(2)}, u32[]{:S(2)}) collective-permute-start(bf16[192,1664]{1,0:T(8,128)(2,1)S(1)} %get-tuple-element.22), channel_id=1, source_target_pairs={{0,1},{1,0},{2,3},{3,2},{4,5},{5,4},{6,7},{7,6},{8,9},{9,8},{10,11... | collective-permute-start | bytes 1916936 | tf_op jit(solution)/shard_map/ppermute | solution.py:288
  75.4 29.4 %collective-permute-start.6 = (bf16[96,1664]{1,0:T(8,128)(2,1)S(1)}, bf16[96,1664]{1,0:T(8,128)(2,1)S(1)}, u32[]{:S(2)}, u32[]{:S(2)}) collective-permute-start(bf16[96,1664]{1,0:T(8,128)(2,1)S(1)} %get-tuple-element.24), channel_id=1, source_target_pairs={{0,2},{2,0},{1,3},{3,1},{4,6},{6,4},{5,7},{7,5},{8,10},{10,8},{9,1... | collective-permute-start | bytes 958472 | tf_op jit(solution)/shard_map/ppermute | solution.py:296
  99.5 3.3 %collective-permute-start.3 = (bf16[192,512]{1,0:T(8,128)(2,1)S(1)}, bf16[192,512]{1,0:T(8,128)(2,1)S(1)}, u32[]{:S(2)}, u32[]{:S(2)}) collective-permute-start(bf16[192,512]{1,0:T(8,128)(2,1)S(1)} %get-tuple-element.18), channel_id=1, source_target_pairs={{0,1},{1,0},{2,3},{3,2},{4,5},{5,4},{6,7},{7,6},{8,9},{9,8},{10,11... | collective-permute-start | bytes 589832 | tf_op jit(solution)/shard_map/ppermute | solution.py:313
  102.9 14.9 %collective-permute-start.4 = (bf16[96,512]{1,0:T(8,128)(2,1)S(1)}, bf16[96,512]{1,0:T(8,128)(2,1)S(1)}, u32[]{:S(2)}, u32[]{:S(2)}) collective-permute-start(bf16[96,512]{1,0:T(8,128)(2,1)S(1)} %get-tuple-element.20), channel_id=1, source_target_pairs={{0,2},{2,0},{1,3},{3,1},{4,6},{6,4},{5,7},{7,5},{8,10},{10,8},{9,1... | collective-permute-start | bytes 294920 | tf_op jit(solution)/shard_map/ppermute | solution.py:321
  134.9 13.4 %copy-start.2 = (s32[128,2]{0,1:T(2,128)S(1)}, s32[128,2]{0,1:T(2,128)}, u32[]{:S(2)}) copy-start(s32[128,2]{0,1:T(2,128)} %param.6) | copy-start | bytes 3076
  135.0 13.5 %copy-start.3 = (bf16[128,2]{0,1:T(2,128)(2,1)S(1)}, bf16[128,2]{0,1:T(2,128)(2,1)}, u32[]{:S(2)}) copy-start(bf16[128,2]{0,1:T(2,128)(2,1)} %param.7) | copy-start | bytes 1540
  135.0 49.7 %all-to-all-start.1 = ((bf16[32,8,2688]{2,1,0:T(8,128)(2,1)}), bf16[32,8,2688]{2,1,0:T(8,128)(2,1)S(1)}, u32[]{:S(2)}, u32[]{:S(2)}) async-start(bf16[32,8,2688]{2,1,0:T(8,128)(2,1)} %bitcast.9), calls=%async_computation.1 | async-start | bytes 2752512 | tf_op jit(solution)/shard_map/all_to_all | solution.py:343
Sparse Core Ops, SparseCore 0:
  56.3 55.9 all-gather.2

commit v6 on v5

--- a/solution.py
+++ b/solution.py
@@ -201,9 +201,11 @@
     half = width // 2
     me = where_ref[2]
     copies = []
-    for i, step in enumerate((0, 3, 1, 2)):
-        source = lax.rem(me + step, 4)
-        copies.append(pltpu.make_async_copy(w_ref.at[source], wbuf.at[pl.ds(i * cols, cols)], sems.at[i]))
+    for j in range(2):
+        for i, step in enumerate((0, 3, 1, 2)):
+            piece = w_ref.at[lax.rem(me + step, 4), :, pl.ds(j * half, half)]
+            to = wbuf.at[pl.ds(i * cols, cols), pl.ds(j * half, half)]
+            copies.append(pltpu.make_async_copy(piece, to, sems.at[4 * j + i]))
     for copy in copies:
         copy.start()
     quarter = hid_ref.shape[0] // 4
@@ -213,11 +215,14 @@
         hb[t * extras : (t + 1) * extras, :] = hid_ref[t * quarter + fulls : (t + 1) * quarter, :]
     low = dot(unfold_rows(4 * extras, 0), hb[...]).astype(BF)
     high = dot(unfold_rows(4 * extras, 1), hb[...]).astype(BF)
-    for copy in copies:
+    for copy in copies[:4]:
         copy.wait()
-    out_ref[:, :width] = dot(ha[...], wbuf[...]).astype(BF)
-    folded = dot(low, wbuf[:, :half]) + dot(high, wbuf[:, half:])
-    out_ref[:, width:] = folded.astype(BF)
+    out_ref[:, :half] = dot(ha[...], wbuf[:, :half]).astype(BF)
+    folded = dot(low, wbuf[:, :half])
+    for copy in copies[4:]:
+        copy.wait()
+    out_ref[:, half:width] = dot(ha[...], wbuf[:, half:]).astype(BF)
+    out_ref[:, width:] = (folded + dot(high, wbuf[:, half:])).astype(BF)
 
 
 def shape(*dims, dtype=BF):
@@ -235,7 +240,7 @@
         out_shape=shape(rows, cols),
         in_specs=[pl.BlockSpec((rows // 2, cols), lambda i: (i, 0))] + [ANY] * len(after),
         out_specs=pl.BlockSpec((rows // 2, cols), lambda i: (i, 0)),
-        cost_estimate=pl.CostEstimate(flops=10000000000, transcendentals=0, bytes_accessed=4 * rows * cols),
+        cost_estimate=pl.CostEstimate(flops=10**10, transcendentals=0, bytes_accessed=4 * rows * cols),
         interpret=INTERPRET,
     )(x, *after)
 
@@ -282,7 +287,7 @@
             pltpu.VMEM((6, width, cols), BF),
             pltpu.SemaphoreType.DMA((3,)),
         ),
-        flops=10 * 12 * slots * width * cols,
+        flops=100 * 12 * slots * width * cols,
         moved=12 << 20,
     )(where, arrived, *map(in_hbm, (own_in, near_in, other_in)))
     got = lax.ppermute(send, "core", swap)
@@ -324,7 +329,7 @@
     )(keep, got, early, scale)
 
     hidden = lax.all_gather(hidden, TENSOR, axis=0, tiled=True)
-    own_out = handed_on(weight_out[0], (near_in, other_in))
+    own_out = handed_on(weight_out[0], (near_in, other_in)) + arrived[:1, :1] * 0
     down = lax.all_gather(own_out, "dp", axis=0)
     sending = kernel_call(
         down_body,
@@ -335,7 +340,7 @@
             pltpu.VMEM((experts * FULL, 4 * cols), BF),
             pltpu.VMEM((experts * EXTRA, 4 * cols), BF),
             pltpu.VMEM((4 * cols, width), BF),
-            pltpu.SemaphoreType.DMA((4,)),
+            pltpu.SemaphoreType.DMA((8,)),
         ),
         flops=4 * experts * FULL * 4 * cols * width,
         moved=6 << 20,

time: 194 us -> 179 us (0.923)
  waiting for transfers between devices: 97 us -> 77.3 us
  blocking collectives: 11.1 us -> 13.6 us
  starting transfers between devices: 49.9 us -> 47.5 us
  other arithmetic: 0.08 us -> 2.25 us
    ppermute x1, waiting for transfers between devices: 17.5 us -> 0.01 us  [per_device(): far_in = lax.ppermute(near_in, ring, forth)]
    all_to_all x1, starting transfers between devices: 13.3 us -> 8.61 us  [per_device(): lax.all_to_all(sending.reshape(experts, FULL, wire), ('z', 'yl'), 0, 0, t...]
    all_gather x1, blocking collectives: 11.1 us -> 13.6 us  [per_device(): hidden = lax.all_gather(hidden, TENSOR, axis=0, tiled=True)]
    ppermute x2, starting transfers between devices: 7.6 us -> 9.81 us  [per_device(): got = lax.ppermute(send, 'yh', swap)]
    add x0 -> x1, other arithmetic: none -> 2.18 us  [per_device(): handed_on(weight_out[0], (near_in, other_in)) + arrived[:1, :1] * 0]
    ppermute x2, waiting for transfers between devices: 12.7 us -> 10.6 us  [per_device(): got = lax.ppermute(send, 'yh', swap)]
  transfers between devices with their start and end apart: 10 -> 10, of which waited for: 7 -> 7; matrix products, arithmetic and copies ran while one was open for 0% -> 2% of each run, Pallas kernels for 6% -> 7%
where the time goes in v6:
time: 179 us; the launch traced here: 178 us
  waiting for transfers between devices  77.3 us (43%)
  starting transfers between devices  47.5 us (27%)
  Pallas kernels  19.5 us (11%)
  between operations  14.2 us (8%)
  blocking collectives  13.6 us (8%)
  local copies, waits for them, and re-layouts  3.76 us (2%)
  other arithmetic  2.25 us (1%)
    all_to_all x1, waiting for transfers between devices, per_device(): lax.all_to_all(sending.reshape(experts, FULL, wire), ('z', 'yl'), 0, 0, t...  36.1 us
    ppermute x1, waiting for transfers between devices, per_device(): near_in = lax.ppermute(own_in, ring, forth)  23.1 us
    all_gather x1, blocking collectives, per_device(): hidden = lax.all_gather(hidden, TENSOR, axis=0, tiled=True)  13.6 us
    ppermute x2, waiting for transfers between devices, per_device(): got = lax.ppermute(send, 'yh', swap)  10.6 us
    all_to_all x1, starting transfers between devices, per_device(): lax.all_to_all(outgoing.reshape(experts, FULL, wire), ('z', 'yl'), 0, 0,...  9.9 us
    ppermute x2, starting transfers between devices, per_device(): got = lax.ppermute(send, 'yh', swap)  9.81 us
    all_to_all x1, starting transfers between devices, per_device(): lax.all_to_all(sending.reshape(experts, FULL, wire), ('z', 'yl'), 0, 0, t...  8.61 us
    ppermute x1, starting transfers between devices, per_device(): near_in = lax.ppermute(own_in, ring, forth)  7.75 us
  transfers between devices with their start and end apart: 10, of which 7 were waited for; matrix products, arithmetic and copies ran while one was open for 2% of the time, Pallas kernels for 7%

profile of v6, /device:TPU:6, one launch (start us, length us, event | category | flops | bytes accessed | tf_op | source)
XLA Modules:
  0.0 178.2 jit_solution(2220076386623028659)
XLA Ops:
  6.5 7.8 %collective-permute-start = (bf16[2,1792,256]{2,1,0:T(8,128)(2,1)}, bf16[2,1792,256]{2,1,0:T(8,128)(2,1)}, u32[]{:S(2)}, u32[]{:S(2)}) collective-permute-start(bf16[2,1792,256]{2,1,0:T(8,128)(2,1)} %bitcast.17), channel_id=1, source_target_pairs={{0,128},{1,385},{128,256},{129,1},{256,384},{257,129},{384,0},{385... | collective-permute-start | bytes 5505032 | tf_op jit(solution)/shard_map/ppermute | solution.py:265
  14.3 1.9 %collective-permute-start.1 = (bf16[2,1792,256]{2,1,0:T(8,128)(2,1)}, bf16[2,1792,256]{2,1,0:T(8,128)(2,1)S(1)}, u32[]{:S(2)}, u32[]{:S(2)}) collective-permute-start(bf16[2,1792,256]{2,1,0:T(8,128)(2,1)} %bitcast.18), channel_id=1, source_target_pairs={{128,0},{385,1},{256,128},{1,129},{384,256},{129,257},{0,384},{257... | collective-permute-start | bytes 5505032 | tf_op jit(solution)/shard_map/ppermute | solution.py:266
  16.2 0.0 copy-start
  16.2 1.0 copy-done
  17.2 0.0 copy-start.1
  17.2 0.7 copy-done.1
  17.9 1.9 %shard_map.55 = bf16[256,2688]{1,0:T(8,128)(2,1)} custom-call(s32[2,128]{1,0:T(2,128)S(1)} %bitcast.15, bf16[128,1792]{1,0:T(8,128)(2,1)S(1)} %copy-done), custom_call_target="tpu_custom_call" | custom-call | flops 234881024 | bytes 4194304 | tf_op jit(solution)/shard_map/pallas_call | solution.py:269
  19.8 9.9 %all-to-all-start = ((bf16[32,8,2688]{2,1,0:T(8,128)(2,1)}), bf16[32,8,2688]{2,1,0:T(8,128)(2,1)S(1)}, u32[]{:S(2)}, u32[]{:S(2)}) async-start(bf16[32,8,2688]{2,1,0:T(8,128)(2,1)} %bitcast.4), calls=%async_computation | async-start | bytes 2752512 | tf_op jit(solution)/shard_map/all_to_all | solution.py:277
  29.7 0.0 all-gather.3.cloned.1.call-start
  29.8 0.1 pad_add_fusion.where_ref
  29.8 23.1 %collective-permute-done.refs_1_.refs_0_ = bf16[2,1792,256]{2,1,0:T(8,128)(2,1)} collective-permute-done((bf16[2,1792,256]{2,1,0:T(8,128)(2,1)}, bf16[2,1792,256]{2,1,0:T(8,128)(2,1)}, u32[]{:S(2)}, u32[]{:S(2)}) %collective-permute-start) | collective-permute-done | bytes 1835040 | tf_op jit(solution)/shard_map/ppermute | solution.py:265
  52.9 5.6 %collective-permute-start.2 = (bf16[2,1792,256]{2,1,0:T(8,128)(2,1)}, bf16[2,1792,256]{2,1,0:T(8,128)(2,1)}, u32[]{:S(2)}, u32[]{:S(2)}) collective-permute-start(bf16[2,1792,256]{2,1,0:T(8,128)(2,1)} %collective-permute-done.refs_1_.refs_0_), channel_id=1, source_target_pairs={{0,128},{1,385},{128,256},{129,1},{256,384},{257,129},{384,0},{385... | collective-permute-start | bytes 5505032 | tf_op jit(solution)/shard_map/ppermute | solution.py:267
  58.5 0.0 collective-permute-done.1.refs_2_.refs_1_
  58.5 0.0 copy-start.4
  58.5 1.3 copy-done.4
  59.8 2.0 %shard_map.62 = bf16[256,1792]{1,0:T(8,128)(2,1)} custom-call(bf16[256,1792]{1,0:T(8,128)(2,1)} %bitcast.20, bf16[2,1792,256]{2,1,0:T(8,128)(2,1)} %collective-permute-done.refs_1_.refs_0_, bf16[2,1792,256]{2,1,0:T(8,128)(2,1)} %copy-done.4), custom_call_target="tpu_custom_call" | custom-call | flops 10000000000 | bytes 1835008 | tf_op jit(solution)/shard_map/pallas_call | solution.py:237
  61.8 4.1 %all-to-all-done = bf16[32,8,2688]{2,1,0:T(8,128)(2,1)S(1)} async-done(((bf16[32,8,2688]{2,1,0:T(8,128)(2,1)}), bf16[32,8,2688]{2,1,0:T(8,128)(2,1)S(1)}, u32[]{:S(2)}, u32[]{:S(2)}) %all-to-all-start) | async-done | bytes 1376288 | tf_op jit(solution)/shard_map/all_to_all | solution.py:277
  65.9 0.5 slice.4
  67.1 2.2 %broadcast_add_fusion = bf16[256,1792]{1,0:T(8,128)(2,1)} fusion(bf16[256,1792]{1,0:T(8,128)(2,1)} %shard_map.62, bf16[]{:T(256)} %bitcast.8), kind=kLoop, calls=%fused_computation | loop fusion | flops 458752 | bytes 1835010 | tf_op jit(solution)/shard_map/add | solution.py:332
  69.3 0.0 all-gather.3.cloned.1.call-update
  69.3 5.1 %shard_map.56 = (bf16[192,1664]{1,0:T(8,128)(2,1)S(1)}, f32[192,1664]{1,0:T(8,128)S(1)}, bf16[384,1792]{1,0:T(8,128)(2,1)S(1)}) custom-call(s32[3]{0:T(128)S(1)} %pad_add_fusion.where_ref, bf16[256,2688]{1,0:T(8,128)(2,1)S(1)} %bitcast.14, bf16[2,1792,256]{2,1,0:T(8,128)(2,1)} %bitcast.19, bf16[2,1792,256]{2,1,0:T(8,128)(2,1)} %collective-permute-done.refs_1_.refs_0_, ...), custom_call_target="tpu_custom_call" | custom-call | flops 211392921600 | bytes 12582912 | tf_op jit(solution)/shard_map/pallas_call | solution.py:280
  74.4 1.9 %collective-permute-start.5 = (bf16[192,1664]{1,0:T(8,128)(2,1)S(1)}, bf16[192,1664]{1,0:T(8,128)(2,1)S(1)}, u32[]{:S(2)}, u32[]{:S(2)}) collective-permute-start(bf16[192,1664]{1,0:T(8,128)(2,1)S(1)} %get-tuple-element.22), channel_id=1, source_target_pairs={{0,1},{1,0},{2,3},{3,2},{4,5},{5,4},{6,7},{7,6},{8,9},{9,8},{10,11... | collective-permute-start | bytes 1916936 | tf_op jit(solution)/shard_map/ppermute | solution.py:293
  76.4 2.0 %collective-permute-done.5.got_ref = bf16[192,1664]{1,0:T(8,128)(2,1)S(1)} collective-permute-done((bf16[192,1664]{1,0:T(8,128)(2,1)S(1)}, bf16[192,1664]{1,0:T(8,128)(2,1)S(1)}, u32[]{:S(2)}, u32[]{:S(2)}) %collective-permute-start.5) | collective-permute-done | bytes 639008 | tf_op jit(solution)/shard_map/ppermute | solution.py:293
  78.4 0.3 shard_map.59
  78.7 5.7 %collective-permute-start.6 = (bf16[96,1664]{1,0:T(8,128)(2,1)S(1)}, bf16[96,1664]{1,0:T(8,128)(2,1)S(1)}, u32[]{:S(2)}, u32[]{:S(2)}) collective-permute-start(bf16[96,1664]{1,0:T(8,128)(2,1)S(1)} %get-tuple-element.24), channel_id=1, source_target_pairs={{0,2},{2,0},{1,3},{3,1},{4,6},{6,4},{5,7},{7,5},{8,10},{10,8},{9,1... | collective-permute-start | bytes 958472 | tf_op jit(solution)/shard_map/ppermute | solution.py:301
  84.4 0.0 collective-permute-done.2.w_ref
  84.4 2.4 %shard_map.57 = (bf16[192,512]{1,0:T(8,128)(2,1)S(1)}, f32[192,512]{1,0:T(8,128)S(1)}) custom-call(bf16[384,1792]{1,0:T(8,128)(2,1)S(1)} %get-tuple-element.16.rows_ref, bf16[2,1792,256]{2,1,0:T(8,128)(2,1)} %collective-permute-done.2.w_ref), custom_call_target="tpu_custom_call" | custom-call | flops 704643072 | bytes 4194304 | tf_op jit(solution)/shard_map/pallas_call | solution.py:310
  86.8 1.9 %collective-permute-start.3 = (bf16[192,512]{1,0:T(8,128)(2,1)S(1)}, bf16[192,512]{1,0:T(8,128)(2,1)S(1)}, u32[]{:S(2)}, u32[]{:S(2)}) collective-permute-start(bf16[192,512]{1,0:T(8,128)(2,1)S(1)} %get-tuple-element.18), channel_id=1, source_target_pairs={{0,1},{1,0},{2,3},{3,2},{4,5},{5,4},{6,7},{7,6},{8,9},{9,8},{10,11... | collective-permute-start | bytes 589832 | tf_op jit(solution)/shard_map/ppermute | solution.py:318
  88.7 1.4 collective-permute-done.3.got_ref
  90.1 4.1 %collective-permute-start.4 = (bf16[96,512]{1,0:T(8,128)(2,1)S(1)}, bf16[96,512]{1,0:T(8,128)(2,1)S(1)}, u32[]{:S(2)}, u32[]{:S(2)}) collective-permute-start(bf16[96,512]{1,0:T(8,128)(2,1)S(1)} %get-tuple-element.20), channel_id=1, source_target_pairs={{0,2},{2,0},{1,3},{3,1},{4,6},{6,4},{5,7},{7,5},{8,10},{10,8},{9,1... | collective-permute-start | bytes 294920 | tf_op jit(solution)/shard_map/ppermute | solution.py:326
  94.3 9.6 %collective-permute-done.6.got_ref = bf16[96,1664]{1,0:T(8,128)(2,1)S(1)} collective-permute-done((bf16[96,1664]{1,0:T(8,128)(2,1)S(1)}, bf16[96,1664]{1,0:T(8,128)(2,1)S(1)}, u32[]{:S(2)}, u32[]{:S(2)}) %collective-permute-start.6) | collective-permute-done | bytes 319520 | tf_op jit(solution)/shard_map/ppermute | solution.py:301
  103.8 0.2 shard_map.60
  104.1 1.1 collective-permute-done.4.got_ref
  105.1 0.1 shard_map.61
  105.3 13.6 %all_gather.9.hid_ref = bf16[384,1024]{1,0:T(8,128)(2,1)S(1)} all-gather(bf16[96,1024]{1,0:T(8,128)(2,1)S(1)} %shard_map.61), channel_id=1, replica_groups=mesh['dp'=4,'z'=8,'yl'=4,'yh'=2,'core'=2] {'yh','core'}, dimensions={0}, use_global_device_ids=true | all-gather | bytes 983040 | tf_op jit(solution)/shard_map/all_gather | solution.py:331
  118.9 0.0 all-gather.3.cloned.1.call-done
  118.9 5.8 %shard_map.63 = bf16[256,2688]{1,0:T(8,128)(2,1)} custom-call(s32[3]{0:T(128)S(1)} %pad_add_fusion.where_ref, bf16[384,1024]{1,0:T(8,128)(2,1)S(1)} %all_gather.9.hid_ref, bf16[4,256,1792]{2,1,0:T(8,128)(2,1)} %bitcast.16), custom_call_target="tpu_custom_call" | custom-call | flops 1879048192 | bytes 6291456 | tf_op jit(solution)/shard_map/pallas_call | solution.py:334
  124.8 0.0 copy-start.2
  124.8 0.0 copy-start.3
  124.8 8.6 %all-to-all-start.1 = ((bf16[32,8,2688]{2,1,0:T(8,128)(2,1)}), bf16[32,8,2688]{2,1,0:T(8,128)(2,1)S(1)}, u32[]{:S(2)}, u32[]{:S(2)}) async-start(bf16[32,8,2688]{2,1,0:T(8,128)(2,1)} %bitcast.10), calls=%async_computation.1 | async-start | bytes 2752512 | tf_op jit(solution)/shard_map/all_to_all | solution.py:348
  133.4 0.0 copy-done.2
  133.4 0.1 copy.6.ids_ref
  133.5 0.0 copy-done.3
  133.5 0.1 copy.7.score_ref
  133.7 36.1 %all-to-all-done.1 = bf16[32,8,2688]{2,1,0:T(8,128)(2,1)S(1)} async-done(((bf16[32,8,2688]{2,1,0:T(8,128)(2,1)}), bf16[32,8,2688]{2,1,0:T(8,128)(2,1)S(1)}, u32[]{:S(2)}, u32[]{:S(2)}) %all-to-all-start.1) | async-done | bytes 1376288 | tf_op jit(solution)/shard_map/all_to_all | solution.py:348
  169.7 1.7 shard_map.64
  (1 shorter events, 0.0 us)
Async XLA Ops:
  6.5 46.3 %collective-permute-start = (bf16[2,1792,256]{2,1,0:T(8,128)(2,1)}, bf16[2,1792,256]{2,1,0:T(8,128)(2,1)}, u32[]{:S(2)}, u32[]{:S(2)}) collective-permute-start(bf16[2,1792,256]{2,1,0:T(8,128)(2,1)} %bitcast.17), channel_id=1, source_target_pairs={{0,128},{1,385},{128,256},{129,1},{256,384},{257,129},{384,0},{385... | collective-permute-start | bytes 5505032 | tf_op jit(solution)/shard_map/ppermute | solution.py:265
  14.3 44.2 %collective-permute-start.1 = (bf16[2,1792,256]{2,1,0:T(8,128)(2,1)}, bf16[2,1792,256]{2,1,0:T(8,128)(2,1)S(1)}, u32[]{:S(2)}, u32[]{:S(2)}) collective-permute-start(bf16[2,1792,256]{2,1,0:T(8,128)(2,1)} %bitcast.18), channel_id=1, source_target_pairs={{128,0},{385,1},{256,128},{1,129},{384,256},{129,257},{0,384},{257... | collective-permute-start | bytes 5505032 | tf_op jit(solution)/shard_map/ppermute | solution.py:266
  16.2 1.0 copy-start
  17.2 0.7 copy-start.1
  19.8 46.1 %all-to-all-start = ((bf16[32,8,2688]{2,1,0:T(8,128)(2,1)}), bf16[32,8,2688]{2,1,0:T(8,128)(2,1)S(1)}, u32[]{:S(2)}, u32[]{:S(2)}) async-start(bf16[32,8,2688]{2,1,0:T(8,128)(2,1)} %bitcast.4), calls=%async_computation | async-start | bytes 2752512 | tf_op jit(solution)/shard_map/all_to_all | solution.py:277
  29.7 89.2 %all-gather.3.cloned.1.call-start = ((), (), s32[]{:S(2)}) async-start(), calls=%async_computation.2 | async-start | bytes 4587520 | tf_op jit(solution)/shard_map/all_gather | solution.py:333
  52.9 31.5 %collective-permute-start.2 = (bf16[2,1792,256]{2,1,0:T(8,128)(2,1)}, bf16[2,1792,256]{2,1,0:T(8,128)(2,1)}, u32[]{:S(2)}, u32[]{:S(2)}) collective-permute-start(bf16[2,1792,256]{2,1,0:T(8,128)(2,1)} %collective-permute-done.refs_1_.refs_0_), channel_id=1, source_target_pairs={{0,128},{1,385},{128,256},{129,1},{256,384},{257,129},{384,0},{385... | collective-permute-start | bytes 5505032 | tf_op jit(solution)/shard_map/ppermute | solution.py:267
  58.5 1.3 copy-start.4
  74.4 4.0 %collective-permute-start.5 = (bf16[192,1664]{1,0:T(8,128)(2,1)S(1)}, bf16[192,1664]{1,0:T(8,128)(2,1)S(1)}, u32[]{:S(2)}, u32[]{:S(2)}) collective-permute-start(bf16[192,1664]{1,0:T(8,128)(2,1)S(1)} %get-tuple-element.22), channel_id=1, source_target_pairs={{0,1},{1,0},{2,3},{3,2},{4,5},{5,4},{6,7},{7,6},{8,9},{9,8},{10,11... | collective-permute-start | bytes 1916936 | tf_op jit(solution)/shard_map/ppermute | solution.py:293
  78.7 25.2 %collective-permute-start.6 = (bf16[96,1664]{1,0:T(8,128)(2,1)S(1)}, bf16[96,1664]{1,0:T(8,128)(2,1)S(1)}, u32[]{:S(2)}, u32[]{:S(2)}) collective-permute-start(bf16[96,1664]{1,0:T(8,128)(2,1)S(1)} %get-tuple-element.24), channel_id=1, source_target_pairs={{0,2},{2,0},{1,3},{3,1},{4,6},{6,4},{5,7},{7,5},{8,10},{10,8},{9,1... | collective-permute-start | bytes 958472 | tf_op jit(solution)/shard_map/ppermute | solution.py:301
  86.8 3.3 %collective-permute-start.3 = (bf16[192,512]{1,0:T(8,128)(2,1)S(1)}, bf16[192,512]{1,0:T(8,128)(2,1)S(1)}, u32[]{:S(2)}, u32[]{:S(2)}) collective-permute-start(bf16[192,512]{1,0:T(8,128)(2,1)S(1)} %get-tuple-element.18), channel_id=1, source_target_pairs={{0,1},{1,0},{2,3},{3,2},{4,5},{5,4},{6,7},{7,6},{8,9},{9,8},{10,11... | collective-permute-start | bytes 589832 | tf_op jit(solution)/shard_map/ppermute | solution.py:318
  90.1 15.0 %collective-permute-start.4 = (bf16[96,512]{1,0:T(8,128)(2,1)S(1)}, bf16[96,512]{1,0:T(8,128)(2,1)S(1)}, u32[]{:S(2)}, u32[]{:S(2)}) collective-permute-start(bf16[96,512]{1,0:T(8,128)(2,1)S(1)} %get-tuple-element.20), channel_id=1, source_target_pairs={{0,2},{2,0},{1,3},{3,1},{4,6},{6,4},{5,7},{7,5},{8,10},{10,8},{9,1... | collective-permute-start | bytes 294920 | tf_op jit(solution)/shard_map/ppermute | solution.py:326
  124.8 8.6 %copy-start.2 = (s32[128,2]{0,1:T(2,128)S(1)}, s32[128,2]{0,1:T(2,128)}, u32[]{:S(2)}) copy-start(s32[128,2]{0,1:T(2,128)} %param.6) | copy-start | bytes 3076
  124.8 8.8 %copy-start.3 = (bf16[128,2]{0,1:T(2,128)(2,1)S(1)}, bf16[128,2]{0,1:T(2,128)(2,1)}, u32[]{:S(2)}) copy-start(bf16[128,2]{0,1:T(2,128)(2,1)} %param.7) | copy-start | bytes 1540
  124.8 44.9 %all-to-all-start.1 = ((bf16[32,8,2688]{2,1,0:T(8,128)(2,1)}), bf16[32,8,2688]{2,1,0:T(8,128)(2,1)S(1)}, u32[]{:S(2)}, u32[]{:S(2)}) async-start(bf16[32,8,2688]{2,1,0:T(8,128)(2,1)} %bitcast.10), calls=%async_computation.1 | async-start | bytes 2752512 | tf_op jit(solution)/shard_map/all_to_all | solution.py:348
Sparse Core Ops, SparseCore 0:
  69.4 43.5 all-gather.2
